TPU v7x, 128 devices: a whole 4x4x4 slice. The times are simulated.
128 devices in a mesh: blk: 16 (over y, x), tp: 8 (over z, core).
Axes of the slice: x: 4, y: 4, z: 4, core: 2. Of those that a mesh axis runs over, the one named last changes fastest.
Arguments:
- hidden_in: bfloat16 [8192, 6144], P('blk', 'tp'), may hold values from -40 to 40
- ln_gain: float32 [6144], replicated, may hold values from 0.1 to 1.9
- w_qkv: bfloat16 [6144, 3, 3072], P(None, None, 'tp'), may hold values from -1 to 1
- w_out: bfloat16 [3072, 6144], P('tp'), may hold values from -0.625 to 0.625
- doc_lengths: int32 [64], replicated, may hold values from 0 to 4096, as said below
- segment_ids: int32 [8192], P('blk'), may hold values from 0 to 63, as said below
- pair_table: int32 [16, 16], replicated, may hold values from 0 to 1, as said below
- page_table: int32 [512], P('blk'), may hold values from 0 to 511, as said below
Outputs:
- attn_out: bfloat16 [8192, 6144], P('blk', 'tp')
- page_cache: bfloat16 [2, 512, 16, 3072], P(None, 'blk', None, 'tp')
Inputs may be any that keep to these rules, and one draw needn't show every extreme that they name: `doc_lengths`: the 64 documents in stream order; they sum to 8192, the empty ones stand just before the last slot, which holds the stream's last document, and the second document has exactly 4096 tokens. segment_ids[t] is the number of documents that end at or before token t; the last token belongs to slot 63. pair_table[i, j] is 1 exactly where a token of block j of 512 tokens and a token at or after it in block i lie in one document. `page_table`: the 32 entries of one block of tokens are that block's own page numbers, each once.
All inputs are finite; a program needn't handle non-finite values.
Results may differ from a plain program's by a relative error of at most 0.014.
Values may be sent and summed in bfloat16 or wider, within the bound.
A program may use at most 256 MiB of HBM per device.

v0:
```python
import jax
import jax.numpy as jnp
from jax import lax
from jax.sharding import PartitionSpec as P

HD = 96
ROT = 24
PAGE = 16


EPSILON = 1e-05


def layer_norm(whole, ln_gain):
    values32 = whole.astype(jnp.float32)
    row_mean = jnp.mean(values32, axis=-1, keepdims=True)
    centred = values32 - row_mean
    row_var = jnp.mean(centred * centred, axis=-1, keepdims=True)
    return (centred * lax.rsqrt(row_var + EPSILON) * ln_gain).astype(jnp.bfloat16)


def doc_positions(token_index, doc_lengths, segment_ids):
    starts = jnp.cumsum(doc_lengths) - doc_lengths
    slots = jnp.arange(doc_lengths.shape[0], dtype=jnp.int32)
    in_document = segment_ids[:, None] == slots[None, :]
    offsets = jnp.sum(jnp.where(in_document, starts[None, :], 0), axis=1)
    return token_index - offsets


def rotary(head_block, positions):
    half_rot = ROT // 2
    frequency = 10000.0 ** (-(2.0 * jnp.arange(half_rot, dtype=jnp.float32)) / ROT)
    angles = positions.astype(jnp.float32)[:, None] * frequency[None, :]
    cosine = jnp.cos(angles)[:, None, :]
    sine_part = jnp.sin(angles)[:, None, :]
    lower_half = head_block[..., :half_rot]
    upper_half = head_block[..., half_rot:ROT]
    return jnp.concatenate(
        [
            lower_half * cosine - upper_half * sine_part,
            upper_half * cosine + lower_half * sine_part,
            head_block[..., ROT:],
        ],
        axis=-1,
    )


def per_device(hidden_in, ln_gain, w_qkv, w_out, doc_lengths, segment_ids, pair_table, page_table):
    row_count = hidden_in.shape[0]
    whole = lax.all_gather(hidden_in, "tp", axis=1, tiled=True)
    normed = layer_norm(whole, ln_gain)
    width = whole.shape[1]
    col_count = w_qkv.shape[2]
    head_count = col_count // HD
    projected = jnp.dot(
        normed, w_qkv.reshape(width, 3 * col_count), preferred_element_type=jnp.float32
    ).reshape(row_count, 3, head_count, HD)
    block_index = lax.axis_index("blk")
    token_index = block_index * row_count + jnp.arange(row_count, dtype=jnp.int32)
    positions = doc_positions(token_index, doc_lengths, segment_ids)
    queries = rotary(projected[:, 0], positions).astype(jnp.bfloat16)
    key_rows = rotary(projected[:, 1], positions).astype(jnp.bfloat16)
    values = projected[:, 2].astype(jnp.bfloat16)
    table_row = lax.dynamic_index_in_dim(pair_table, block_index, 0, keepdims=False)
    block_ids = jnp.arange(pair_table.shape[1], dtype=jnp.int32)
    scale = HD ** (-0.5)
    start_state = (
        jnp.full((head_count, row_count), -1e30, jnp.float32),
        jnp.zeros((head_count, row_count), jnp.float32),
        jnp.zeros((head_count, row_count, HD), jnp.float32),
    )
    key_piece = lax.all_gather(key_rows, "blk", axis=0, tiled=True)
    value_piece = lax.all_gather(values, "blk", axis=0, tiled=True)
    segment_piece = lax.all_gather(segment_ids, "blk", axis=0, tiled=True)
    piece_rows = key_piece.shape[0]
    key_index = jnp.arange(piece_rows, dtype=jnp.int32)
    matches = (key_index // row_count)[:, None] == block_ids[None, :]
    live = jnp.sum(jnp.where(matches, table_row[None, :], 0), axis=1) > 0

    def compute(previous):
        maxima, totals, weighted = previous
        scores = (
            jnp.einsum("qhd,khd->hqk", queries, key_piece, preferred_element_type=jnp.float32)
            * scale
        )
        allowed = (
            live[None, :]
            & (segment_ids[:, None] == segment_piece[None, :])
            & (key_index[None, :] <= token_index[:, None])
        )
        scores = jnp.where(allowed[None], scores, -jnp.inf)
        newest = jnp.maximum(maxima, jnp.max(scores, axis=-1))
        weights = jnp.exp(scores - newest[..., None])
        totals = jnp.sum(weights, axis=-1)
        weighted = jnp.einsum(
            "hqk,khd->hqd",
            weights.astype(jnp.bfloat16),
            value_piece,
            preferred_element_type=jnp.float32,
        )
        return (newest, totals, weighted)

    final = lax.cond(jnp.any(live), compute, lambda previous: previous, start_state)
    mixed = (final[2] / final[1][..., None]).astype(jnp.bfloat16)
    heads_out = jnp.transpose(mixed, (1, 0, 2)).reshape(row_count, col_count)
    partial_term = jnp.dot(heads_out, w_out, preferred_element_type=jnp.float32)
    attn_out = lax.psum_scatter(
        partial_term.astype(jnp.bfloat16), "tp", scatter_dimension=1, tiled=True
    )
    page_count = row_count // PAGE
    local_pages = page_table - block_index * page_count
    stacked = jnp.stack(
        [key_rows.reshape(page_count, PAGE, col_count), values.reshape(page_count, PAGE, col_count)]
    )
    page_cache = jnp.zeros_like(stacked).at[:, local_pages].set(stacked)
    return (attn_out, page_cache)


def solution(mesh):
    placed = (P("blk", "tp"), P(), P(None, None, "tp"), P("tp", None), P(), P("blk"), P(), P("blk"))
    return jax.shard_map(
        per_device,
        mesh=mesh,
        in_specs=placed,
        out_specs=(P("blk", "tp"), P(None, "blk", None, "tp")),
        check_vma=False,
    )
```

profile of v0, /device:TPU:1, one launch (start us, length us, event | category | flops | bytes accessed | tf_op | source)
XLA Modules:
  0.0 351.7 jit_solution(17223538342270474863)
XLA Ops:
  7.2 0.0 copy-start
  7.2 0.0 all-gather.6.cloned.1.call-start
  7.2 0.7 all-gather.6.cloned.1.call-update
  7.9 0.0 all-gather.8.cloned.1.call-start
  8.0 0.0 copy-start.7
  8.0 0.0 copy-start.6
  8.0 18.8 %copy.23 = bf16[6144,3,384]{0,2,1:T(8,128)(2,1)} copy(bf16[6144,3,384]{2,0,1:T(8,128)(2,1)} %param.12) | data formatting | bytes 28311552 | tf_op args[2]
  26.8 0.0 copy-start.8
  26.8 0.0 copy-done.7
  26.8 0.1 copy.24
  26.9 0.1 reduce-window.9
  27.0 0.1 reduce
  27.1 0.0 copy-done.6
  27.1 0.1 select_reduce_fusion.1
  27.2 0.2 multiply_cosine_fusion
  27.4 26.9 %all-gather.6.cloned.1.call-done = bf16[512,6144]{1,0:T(8,128)(2,1)} async-done(((bf16[512,768]{1,0:T(8,128)(2,1)}), bf16[512,6144]{1,0:T(8,128)(2,1)}) %all-gather.6.cloned.1.call-update) | async-done | bytes 6291472 | tf_op jit(solution)/shard_map/all_gather | solution.py:50
  54.4 0.0 copy-start.2
  54.4 3.8 %convert_reduce_fusion = f32[512]{0:T(512)S(1)} fusion(bf16[512,6144]{1,0:T(8,128)(2,1)} %all-gather.6.cloned.1.call-done), kind=kLoop, calls=%fused_computation.14 | loop fusion | flops 6290944 | bytes 6293504 | tf_op jit(solution)/shard_map/reduce_sum | solution.py:16
  58.2 4.6 %fusion.10 = f32[512]{0:T(512)S(1)} fusion(bf16[512,6144]{1,0:T(8,128)(2,1)} %all-gather.6.cloned.1.call-done, f32[512]{0:T(512)S(1)} %broadcast_multiply_fusion), kind=kLoop, calls=%fused_computation.17 | loop fusion | flops 12582400 | bytes 6295552 | tf_op jit(solution)/shard_map/reduce_sum | solution.py:18
  62.8 0.0 copy-done.8
  62.8 0.0 copy-done.2
  62.8 11.8 %fusion.14 = f32[512,3,4,96]{0,3,2,1:T(8,128)S(1)} fusion(bf16[3,4,96,6144]{3,2,1,0:T(8,128)(2,1)} %bitcast.33, bf16[512,6144]{1,0:T(8,128)(2,1)S(1)} %copy-done.2, f32[6144]{0:T(1024)S(1)} %copy-done.8, f32[512]{0:T(512)S(1)} %add_rsqrt_fusion, f32[512]{0:T(512)S(1)} %broadcast_multiply_fusion), kind=kOutput, calls=%fused_computation.22 | convolution fusion | flops 7263485952 | bytes 22835200 | tf_op jit(solution)/shard_map/dot_general | solution.py:55
  74.7 0.1 slice_bitcast_fusion
  74.9 0.8 maximum_convert_fusion
  75.7 0.0 all-gather.8.cloned.1.call-update
  75.7 0.0 all-gather.10.cloned.1.call-start
  75.8 0.8 slice.58
  76.6 0.0 all-gather.10.cloned.1.call-update
  76.6 0.0 reduce-scatter.2.cloned.1.call-start
  76.6 0.0 copy-done
  76.7 0.2 select_reduce_fusion
  76.9 0.6 fusion.22
  78.2 19.2 %all-gather.1 = s32[16,1,512]{2,1,0:T(1,128)S(1)} all-gather(s32[1,1,512]{2,1,0:T(1,128)S(1)} %bitcast.36), channel_id=1, replica_groups=mesh['blk'=16,'tp'=8] {'blk'}, dimensions={0}, use_global_device_ids=true | all-gather | bytes 34816 | tf_op jit(solution)/shard_map/all_gather | solution.py:74
  97.5 43.4 %all-gather.8.cloned.1.call-done = bf16[8192,4,96]{0,2,1:T(8,128)(2,1)} async-done(((bf16[512,4,96]{0,2,1:T(8,128)(2,1)}), bf16[8192,4,96]{0,2,1:T(8,128)(2,1)}) %all-gather.8.cloned.1.call-update) | async-done | bytes 6291472 | tf_op jit(solution)/shard_map/all_gather | solution.py:72
  140.9 68.3 %all-gather.10.cloned.1.call-done = bf16[8192,1,4,96]{0,3,2,1:T(8,128)(2,1)} async-done(((bf16[512,1,4,96]{0,3,2,1:T(8,128)(2,1)}), bf16[8192,1,4,96]{0,3,2,1:T(8,128)(2,1)}) %all-gather.10.cloned.1.call-update) | async-done | bytes 6291472 | tf_op jit(solution)/shard_map/all_gather | solution.py:73
  209.2 85.0 %conditional.1 = (f32[4,512]{1,0:T(4,128)S(1)}, f32[4,512,96]{1,2,0:T(8,128)S(1)}) conditional(s32[]{:T(128)} %convert_element_type.56, () %tuple.16, (pred[8192]{0:T(1024)(128)(4,1)S(1)}, s32[512]{0:T(512)S(1)}, s32[8192]{0:T(1024)S(1)}, s32[8192]{0:T(1024)S(1)}, s32[]{:T(128)}, /*index=5*/s32[512]{0:T(512)S(1)}, bf16[512,4,96]{0,2,1:T(8,128)(2,1)S(1)}, ...), branch_computations={%region_6.7_spmd, %region_7.10_spmd} | conditional | flops 6643776000 | bytes 231997456 | solution.py:103
  209.2 5.8 %compare_and_fusion = pred[512,8192]{1,0:T(8,128)(4,1)} fusion(s32[8192]{0:T(1024)S(1)} %get-tuple-element.23, s32[8192]{0:T(1024)S(1)} %get-tuple-element.22, s32[512]{0:T(512)S(1)} %broadcast_add_fusion, s32[512]{0:T(512)S(1)} %get-tuple-element.21, pred[8192]{0:T(1024)(128)(4,1)S(1)} %get-tuple-element.20), kind=kLoop, calls=%fused_computation.8 | loop fusion | flops 16777216 | bytes 4272128 | tf_op jit(solution)/shard_map/cond/branch_1_fun/and | solution.py:87
  215.0 28.2 %fusion = (f32[4,512]{1,0:T(4,128)S(1)}, f32[4,512,8192]{2,1,0:T(8,128)}) fusion(pred[512,8192]{1,0:T(8,128)(4,1)} %compare_and_fusion, bf16[512,4,96]{0,2,1:T(8,128)(2,1)S(1)} %get-tuple-element.26, bf16[8192,4,96]{0,2,1:T(8,128)(2,1)} %get-tuple-element.27), kind=kOutput, calls=%fused_computation.3 | convolution fusion | flops 3271555072 | bytes 77996032 | tf_op jit(solution)/shard_map/cond/branch_1_fun/qhd,khd->hqk/dot_general | solution.py:83
  243.2 28.1 %fusion.3 = f32[4,512,96]{1,2,0:T(8,128)S(1)} fusion(bf16[8192,4,96]{0,2,1:T(8,128)(2,1)} %get-tuple-element.28, f32[4,512,8192]{2,1,0:T(8,128)} %get-tuple-element.38, f32[4,512]{1,0:T(4,128)S(1)} %broadcast_maximum_fusion, pred[512,8192]{1,0:T(8,128)(4,1)} %compare_and_fusion), kind=kOutput, calls=%fused_computation.6 | convolution fusion | flops 3288334336 | bytes 78389248 | tf_op jit(solution)/shard_map/cond/branch_1_fun/hqk,khd->hqd/dot_general | solution.py:95
  271.3 22.7 %fusion.2 = f32[4,512]{1,0:T(4,128)S(1)} fusion(f32[4,512,8192]{2,1,0:T(8,128)} %get-tuple-element.38, f32[4,512]{1,0:T(4,128)S(1)} %broadcast_maximum_fusion, pred[512,8192]{1,0:T(8,128)(4,1)} %compare_and_fusion), kind=kLoop, calls=%fused_computation.5 | loop fusion | flops 67106816 | bytes 71319552 | tf_op jit(solution)/shard_map/cond/branch_1_fun/reduce_sum | solution.py:94
  294.2 0.0 copy-start.9
  294.2 0.0 copy-start.3
  294.3 0.0 copy-start.4
  294.3 0.1 divide_convert_fusion
  294.4 0.0 copy-start.1
  294.4 7.8 %convolution_convert_fusion = bf16[512,6144]{1,0:T(8,128)(2,1)} fusion(bf16[512,384]{0,1:T(8,128)(2,1)S(1)} %bitcast.34, bf16[384,6144]{1,0:T(8,128)(2,1)} %param.13), kind=kOutput, calls=%fused_computation.20 | convolution fusion | flops 2419064832 | bytes 11403264 | tf_op jit(solution)/shard_map/dot_general | solution.py:106
  302.2 0.0 reduce-scatter.2.cloned.1.call-update
  302.2 0.0 copy-done.9
  302.2 0.0 copy-done.3
  302.2 0.3 copy.25
  302.6 0.0 copy-done.4
  302.6 0.3 copy.26
  302.9 0.4 convert_element_type.65
  303.3 0.4 convert_element_type.66
  303.6 0.1 maximum_bitcast_fusion
  303.7 0.1 copy.27
  303.8 0.1 broadcast_in_dim.63
  303.9 2.3 scatter_fusion
  306.2 0.0 copy-start.5
  306.2 38.9 %reduce-scatter.2.cloned.1.call-done = bf16[512,768]{1,0:T(8,128)(2,1)} async-done(((bf16[512,6144]{1,0:T(8,128)(2,1)}), bf16[512,768]{1,0:T(8,128)(2,1)}) %reduce-scatter.2.cloned.1.call-update) | async-done | bytes 786448 | tf_op jit(solution)/shard_map/reduce_scatter | solution.py:107
  345.2 0.0 copy-done.5
  345.2 0.0 copy-done.1
  (17 shorter events, 0.3 us)
Async XLA Ops:
  7.2 69.5 %copy-start = (s32[16,16]{1,0:T(8,128)S(1)}, s32[16,16]{1,0:T(8,128)}, u32[]{:S(2)}) copy-start(s32[16,16]{1,0:T(8,128)} %param.16) | copy-start | bytes 3076
  7.2 47.2 %all-gather.6.cloned.1.call-start = ((), (), s32[]{:S(2)}) async-start(), calls=%async_computation.1 | async-start | bytes 7077888 | tf_op jit(solution)/shard_map/all_gather | solution.py:50
  7.9 133.0 %all-gather.8.cloned.1.call-start = ((), (), s32[]{:S(2)}) async-start(), calls=%async_computation.2 | async-start | bytes 6684672 | tf_op jit(solution)/shard_map/all_gather | solution.py:72
  8.0 18.8 %copy-start.7 = (s32[64]{0:T(128)S(1)}, s32[64]{0:T(128)}, u32[]{:S(2)}) copy-start(s32[64]{0:T(128)} %param.14) | copy-start | bytes 772
  8.0 19.2 %copy-start.6 = (s32[512]{0:T(512)S(1)}, s32[512]{0:T(512)}, u32[]{:S(2)}) copy-start(s32[512]{0:T(512)} %param.15) | copy-start | bytes 6148
  26.8 36.0 %copy-start.8 = (f32[6144]{0:T(1024)S(1)}, f32[6144]{0:T(1024)}, u32[]{:S(2)}) copy-start(f32[6144]{0:T(1024)} %param.11) | copy-start | bytes 73732
  54.4 8.4 %copy-start.2 = (bf16[512,6144]{1,0:T(8,128)(2,1)S(1)}, bf16[512,6144]{1,0:T(8,128)(2,1)}, u32[]{:S(2)}) copy-start(bf16[512,6144]{1,0:T(8,128)(2,1)} %all-gather.6.cloned.1.call-done) | copy-start | bytes 18874372
  75.7 133.5 %all-gather.10.cloned.1.call-start = ((), (), s32[]{:S(2)}) async-start(), calls=%async_computation.4 | async-start | bytes 6684672 | tf_op jit(solution)/shard_map/all_gather | solution.py:73
  76.6 268.6 %reduce-scatter.2.cloned.1.call-start = ((), (), s32[]{:S(2)}) async-start(), calls=%async_computation.3 | async-start | bytes 7077888 | tf_op jit(solution)/shard_map/reduce_scatter | solution.py:107
  294.2 8.0 %copy-start.9 = (s32[32]{0:T(128)S(1)}, s32[32]{0:T(128)}, u32[]{:S(2)}) copy-start(s32[32]{0:T(128)} %param.17) | copy-start | bytes 388
  294.2 8.0 %copy-start.3 = (bf16[512,4,96]{0,2,1:T(8,128)(2,1)S(1)}, bf16[512,4,96]{0,2,1:T(8,128)(2,1)}, u32[]{:S(2)}) copy-start(bf16[512,4,96]{0,2,1:T(8,128)(2,1)} %maximum_convert_fusion) | copy-start | bytes 1179652
  294.3 8.3 %copy-start.4 = (bf16[512,1,4,96]{0,3,2,1:T(8,128)(2,1)S(1)}, bf16[512,1,4,96]{0,3,2,1:T(8,128)(2,1)}, u32[]{:S(2)}) copy-start(bf16[512,1,4,96]{0,3,2,1:T(8,128)(2,1)} %slice.58) | copy-start | bytes 1179652
  294.4 50.8 %copy-start.1 = (s32[16,16]{1,0:T(8,128)S(1)}, s32[16,16]{1,0:T(8,128)}, u32[]{:S(2)}) copy-start(s32[16,16]{1,0:T(8,128)} %param.16) | copy-start | bytes 3076
  306.2 38.9 %copy-start.5 = (bf16[2,32,16,384]{3,2,1,0:T(8,128)(2,1)}, bf16[2,32,16,384]{3,2,1,0:T(8,128)(2,1)S(1)}, u32[]{:S(2)}) copy-start(bf16[2,32,16,384]{3,2,1,0:T(8,128)(2,1)S(1)} %scatter_fusion) | copy-start | bytes 2359300
Sparse Core Ops, SparseCore 0:
  9.7 44.6 all-gather.5
  75.8 64.9 all-gather.7
  143.0 66.1 all-gather.9
  302.3 42.7 reduce-scatter.1
where the time goes:
time: 352 us
  waiting for transfers between devices  178 us (51%)
  matrix products  75.9 us (22%)
  other arithmetic  39.4 us (11%)
  local copies, waits for them, and re-layouts  23.8 us (7%)
  blocking collectives  19.2 us (5%)
  between operations  14.7 us (4%)
    all_gather x1, waiting for transfers between devices, per_device(): value_piece = lax.all_gather(values, 'blk', axis=0, tiled=True)  68.3 us
    all_gather x1, waiting for transfers between devices, per_device(): key_piece = lax.all_gather(key_rows, 'blk', axis=0, tiled=True)  43.4 us
    reduce_scatter x1, waiting for transfers between devices, per_device(): lax.psum_scatter(partial_term.astype(jnp.bfloat16), 'tp', scatter_dimensi...  38.9 us
    dot_general x1, matrix products, compute(): jnp.einsum('qhd,khd->hqk', queries, key_piece, preferred_element_type=jnp...  28.2 us
    dot_general x1, matrix products, compute(): jnp.einsum('hqk,khd->hqd', weights.astype(jnp.bfloat16), value_piece, pre...  28.1 us
    all_gather x1, waiting for transfers between devices, per_device(): whole = lax.all_gather(hidden_in, 'tp', axis=1, tiled=True)  26.9 us
    reduce_sum x1, other arithmetic, compute(): totals = jnp.sum(weights, axis=-1)  22.7 us
    all_gather x1, blocking collectives, per_device(): segment_piece = lax.all_gather(segment_ids, 'blk', axis=0, tiled=True)  19.2 us
  transfers between devices with their start and end apart: 4, of which 4 were waited for; matrix products, arithmetic and copies ran while one was open for 7% of the time, Pallas kernels for 0%

commit v1 on v0

v1 whole, which is shorter than its diff:
```python
import functools

import jax
import jax.numpy as jnp
from jax import lax
from jax.experimental import pallas as pl
from jax.experimental.pallas import tpu as pltpu
from jax.sharding import PartitionSpec as P

HD = 96
ROT = 24
PAGE = 16
ROWS = 512
HALF = 256
SHARD = 768
COLS = 384
EPSILON = 1e-05
LOG2E = 1.4426950408889634
MESH = pl.DeviceIdType.MESH


def remote(src, dst, send, recv, where):
    return pltpu.make_async_remote_copy(
        src_ref=src, dst_ref=dst, send_sem=send, recv_sem=recv, device_id=where, device_id_type=MESH
    )


def project_kernel(
    hid_ref, gain_ref, table_ref, w_ref, out_ref,
    gathered, wbuf, acc, stats, columns, normed,
    w_sem, own_sem, stat_send, stat_recv, ici_send, ici_recv, sib_send, sib_recv,
):
    b = lax.axis_index("blk")
    t = lax.axis_index("tp")
    z, c = t // 2, t % 2
    sibling = (b, z * 2 + 1 - c)
    after = (b, ((z + 1) % 4) * 2 + c)
    before = (b, ((z + 3) % 4) * 2 + c)

    def origin(dz, k):
        return ((z + dz + 4) % 4) * 2 + (c + k) % 2

    order = [(0, 0), (0, 1), (3, 0), (1, 0), (3, 1), (1, 1), (2, 0), (2, 1)]
    loads = []
    for i, (dz, k) in enumerate(order):
        rows = pl.ds(pl.multiple_of(origin(dz, k) * SHARD, SHARD), SHARD)
        copy = pltpu.make_async_copy(w_ref.at[:, rows, :], wbuf.at[:, rows, :], w_sem.at[i])
        copy.start()
        loads.append(copy)
    own_copy = pltpu.make_async_copy(hid_ref, gathered.at[t], own_sem)
    own_copy.start()

    x = hid_ref[...].astype(jnp.float32)
    mean = jnp.sum(x, axis=1, keepdims=True) * (1.0 / SHARD)
    centred = x - mean
    spread = jnp.sum(centred * centred, axis=1, keepdims=True)
    lane = lax.broadcasted_iota(jnp.int32, (ROWS, 128), 1)
    both = jnp.where(lane == 0, mean, spread)
    stats[t] = jnp.transpose(both)[:8]

    barrier = pltpu.get_barrier_semaphore()
    for d in range(1, 8):
        pl.semaphore_signal(barrier, inc=1, device_id=(b, (t + d) % 8), device_id_type=MESH)
    pl.semaphore_wait(barrier, 7)

    a_rows, b_rows = pl.ds(0, HALF), pl.ds(HALF, HALF)

    def piece(who, rows):
        return gathered.at[who, rows]

    stat_copies = []
    for d in range(1, 8):
        copy = remote(stats.at[t], stats.at[t], stat_send.at[d - 1], stat_recv.at[d - 1], (b, (t + d) % 8))
        copy.start()
        stat_copies.append(copy)
    plus = [
        remote(hid_ref.at[a_rows], piece(t, a_rows), ici_send.at[0], ici_recv.at[0], after),
        remote(hid_ref.at[b_rows], piece(t, b_rows), ici_send.at[1], ici_recv.at[1], after),
        remote(piece(origin(3, 0), a_rows), piece(origin(3, 0), a_rows), ici_send.at[2], ici_recv.at[2], after),
    ]
    minus = [
        remote(hid_ref.at[b_rows], piece(t, b_rows), ici_send.at[3], ici_recv.at[3], before),
        remote(hid_ref.at[a_rows], piece(t, a_rows), ici_send.at[4], ici_recv.at[4], before),
        remote(piece(origin(1, 0), b_rows), piece(origin(1, 0), b_rows), ici_send.at[5], ici_recv.at[5], before),
    ]
    across = [remote(hid_ref, gathered.at[t], sib_send.at[0], sib_recv.at[0], sibling)]
    for i, (dz, rows) in enumerate(
        [(3, a_rows), (1, b_rows), (3, b_rows), (1, a_rows), (2, a_rows), (2, b_rows)]
    ):
        who = origin(dz, 0)
        across.append(remote(piece(who, rows), piece(who, rows), sib_send.at[i + 1], sib_recv.at[i + 1], sibling))
    plus[0].start()
    minus[0].start()
    across[0].start()
    plus[1].start()
    minus[1].start()

    acc[...] = jnp.zeros_like(acc)
    for copy in stat_copies:
        copy.wait_recv()
    means = stats[:, 0, :]
    whole_mean = jnp.sum(means, axis=0, keepdims=True) * 0.125
    off = means - whole_mean
    total = jnp.sum(stats[:, 1, :], axis=0, keepdims=True) + SHARD * jnp.sum(off * off, axis=0, keepdims=True)
    inverse = lax.rsqrt(total * (1.0 / (8 * SHARD)) + EPSILON)
    columns[0] = jnp.transpose(jnp.broadcast_to(whole_mean, (128, ROWS)))
    columns[1] = jnp.transpose(jnp.broadcast_to(inverse, (128, ROWS)))

    def compute(who, half):
        start = half * HALF

        def normalise(i, carry):
            rows = pl.ds(pl.multiple_of(start + i * 64, 64), 64)
            here = pl.ds(pl.multiple_of(i * 64, 64), 64)
            centre, scale = columns[0, rows, :], columns[1, rows, :]
            for j in range(SHARD // 128):
                span = slice(128 * j, 128 * j + 128)
                value = gathered[who, rows, span].astype(jnp.float32)
                gain = gain_ref[who, :, span]
                normed[here, span] = ((value - centre) * scale * gain).astype(jnp.bfloat16)
            return carry

        lax.fori_loop(0, HALF // 64, normalise, 0)
        rows = pl.ds(start, HALF)
        depth = pl.ds(pl.multiple_of(who * SHARD, SHARD), SHARD)

        def multiply(kind, carry):
            acc[kind, rows, :] += jnp.dot(
                normed[...], wbuf[kind, depth, :], preferred_element_type=jnp.float32
            )
            return carry

        lax.fori_loop(0, 3, multiply, 0)

    own_copy.wait()
    loads[0].wait()
    compute(t, 0)
    compute(t, 1)
    loads[1].wait()
    across[0].wait_recv()
    compute(origin(0, 1), 0)
    compute(origin(0, 1), 1)

    plus[0].wait_recv()
    plus[2].start()
    across[1].start()
    minus[0].wait_recv()
    minus[2].start()
    across[2].start()
    loads[2].wait()
    compute(origin(3, 0), 0)
    loads[3].wait()
    compute(origin(1, 0), 1)
    loads[4].wait()
    across[1].wait_recv()
    compute(origin(3, 1), 0)
    loads[5].wait()
    across[2].wait_recv()
    compute(origin(1, 1), 1)

    plus[1].wait_recv()
    across[3].start()
    minus[1].wait_recv()
    across[4].start()
    compute(origin(3, 0), 1)
    compute(origin(1, 0), 0)
    across[3].wait_recv()
    compute(origin(3, 1), 1)
    across[4].wait_recv()
    compute(origin(1, 1), 0)

    plus[2].wait_recv()
    across[5].start()
    minus[2].wait_recv()
    across[6].start()
    loads[6].wait()
    compute(origin(2, 0), 0)
    compute(origin(2, 0), 1)
    loads[7].wait()
    across[5].wait_recv()
    compute(origin(2, 1), 0)
    across[6].wait_recv()
    compute(origin(2, 1), 1)

    cosine, sine = table_ref[0], table_ref[1]
    for kind in range(3):
        turned = jnp.transpose(acc[kind])
        for h in range(COLS // HD):
            part = turned[h * HD:(h + 1) * HD]
            if kind < 2:
                head = part[:ROT]
                swapped = jnp.concatenate([head[ROT // 2:], head[:ROT // 2]], axis=0)
                part = jnp.concatenate([head * cosine + swapped * sine, part[ROT:]], axis=0)
            out_ref[h, kind] = part.astype(jnp.bfloat16)

    for copy in stat_copies + plus + minus + across:
        copy.wait_send()


def attend_kernel(
    qkv_ref, low_ref, dest_ref, out_ref, page_ref,
    qbuf, kv, keys, peak, total, acc, done,
    own_sem, kv_send, kv_recv, q_send, q_recv, ag_send, ag_recv, o_send, o_recv,
):
    b = lax.axis_index("blk")
    t = lax.axis_index("tp")
    y, x, c = b // 4, b % 4, t % 2
    mine = (1 - c) * y + c * x
    group = (1 - c) * x + c * y

    def block_of(a, g):
        return (1 - c) * (a * 4 + g) + c * (g * 4 + a)

    barrier = pltpu.get_barrier_semaphore()
    for d in range(1, 4):
        for where in (block_of((mine + d) % 4, group), block_of(mine, (group + d) % 4)):
            pl.semaphore_signal(barrier, inc=1, device_id=(where, t), device_id_type=MESH)
    pl.semaphore_wait(barrier, 6)

    both = pl.ds(1, 2)
    kept = pltpu.make_async_copy(qkv_ref.at[mine, both], kv.at[group, mine], own_sem.at[0])
    kept_q = pltpu.make_async_copy(qkv_ref.at[mine, 0], qbuf.at[mine], own_sem.at[1])
    kept.start()
    kept_q.start()
    sends, q_copies, kv_copies = [], [], []
    order = (1, 3, 2)
    for d in order:
        head = (mine + d) % 4
        copy = remote(
            qkv_ref.at[head, both], kv.at[group, mine], kv_send.at[d - 1], kv_recv.at[d - 1],
            (block_of(head, group), t),
        )
        copy.start()
        kv_copies.append(copy)
    ag_copies = []
    for d in order:
        copy = remote(
            qkv_ref.at[mine, both], kv.at[group, mine], ag_send.at[0, d - 1], ag_recv.at[0, d - 1],
            (block_of(mine, (group + d) % 4), t),
        )
        copy.start()
        ag_copies.append(copy)
    for d in order:
        head = (mine + d) % 4
        copy = remote(
            qkv_ref.at[head, 0], qbuf.at[mine], q_send.at[d - 1], q_recv.at[d - 1],
            (block_of(head, group), t),
        )
        copy.start()
        q_copies.append(copy)

    for d, arrived in zip(order, kv_copies):
        arrived.wait_recv()
        slot = (mine + 4 - d) % 4
        for e in order:
            copy = remote(
                kv.at[group, slot], kv.at[group, slot], ag_send.at[d, e - 1], ag_recv.at[d, e - 1],
                (block_of(mine, (group + e) % 4), t),
            )
            copy.start()
            ag_copies.append(copy)

    spots = lax.broadcasted_iota(jnp.int32, (ROWS, ROWS), 0)
    chosen = (spots == dest_ref[...]).astype(jnp.float32).astype(jnp.bfloat16)
    for kind in range(2):
        source = jnp.concatenate([qkv_ref[h, kind + 1] for h in range(4)], axis=0)
        page_ref[kind] = lax.dot_general(
            chosen, source, (((1,), (1,)), ((), ())), preferred_element_type=jnp.float32
        ).astype(jnp.bfloat16)

    kept.wait()
    kept_q.wait()
    for copy in q_copies + ag_copies:
        copy.wait_recv()

    def turn(i, carry):
        keys[i // 4, i % 4] = jnp.transpose(kv[i // 4, i % 4, 0].astype(jnp.float32)).astype(jnp.bfloat16)
        return carry

    lax.fori_loop(0, 16, turn, 0)

    factor = LOG2E * HD ** (-0.5)
    depth_index = lax.broadcasted_iota(jnp.int32, (ROWS, ROWS), 0)
    o_copies = []
    for step in range(4):
        slot = (mine + 1 + step) % 4
        query_block = block_of(slot, group)
        low = low_ref[query_block]
        query = qbuf[slot]

        def attend(key_block, first):
            a = (1 - c) * (key_block // 4) + c * (key_block % 4)
            g = (1 - c) * (key_block % 4) + c * (key_block // 4)
            score = jnp.dot(keys[g, a], query, preferred_element_type=jnp.float32)
            allowed = depth_index >= low - key_block * ROWS
            if first:
                allowed = allowed & (depth_index <= lax.broadcasted_iota(jnp.int32, (ROWS, ROWS), 1))
            score = jnp.where(allowed, score, -1e30)
            highest = jnp.max(score, axis=0, keepdims=True)
            if not first:
                highest = jnp.maximum(highest, peak[...])
            weight = jnp.exp2((score - highest) * factor)
            added = jnp.sum(weight, axis=0, keepdims=True)
            mixed = jnp.dot(kv[g, a, 1], weight.astype(jnp.bfloat16), preferred_element_type=jnp.float32)
            if first:
                total[...] = added
                acc[...] = mixed
            else:
                fade = jnp.exp2((peak[...] - highest) * factor)
                total[...] = total[...] * fade + added
                acc[...] = acc[...] * fade + mixed
            peak[...] = highest

        attend(query_block, True)

        def older(r, carry):
            key_block = query_block - 1 - r

            @pl.when(key_block >= 0)
            def _():
                attend(key_block, False)

            return carry

        lax.fori_loop(0, 8, older, 0)
        result = (acc[...] / total[...]).astype(jnp.bfloat16)
        if step < 3:
            done[slot] = result
            copy = remote(
                done.at[slot], out_ref.at[mine], o_send.at[step], o_recv.at[step], (block_of(slot, group), t)
            )
            copy.start()
            o_copies.append(copy)
        else:
            out_ref[mine] = result

    for copy in o_copies:
        copy.wait_recv()
    for copy in kv_copies + q_copies + ag_copies + o_copies:
        copy.wait_send()


def output_kernel(
    o_ref, w_ref, out_ref,
    wbuf, x, sib_out, sib_in, tx, rx, w_sem, sib_send, sib_recv, send, recv,
):
    b = lax.axis_index("blk")
    t = lax.axis_index("tp")
    z, c = t // 2, t % 2
    sibling = (b, z * 2 + 1 - c)
    after = (b, ((z + 1) % 4) * 2 + c)
    before = (b, ((z + 3) % 4) * 2 + c)
    order = (2, 1, 3, 0)

    def owner(dz, k):
        return ((z + dz) % 4) * 2 + (c + k) % 2

    loads = {}
    for i, key in enumerate([(2, 1), (2, 0), (1, 1), (1, 0), (3, 1), (3, 0), (0, 1), (0, 0)]):
        who = owner(*key)
        span = pl.ds(pl.multiple_of(who * SHARD, SHARD), SHARD)
        loads[key] = pltpu.make_async_copy(w_ref.at[:, span], wbuf.at[who], w_sem.at[i])
        loads[key].start()

    barrier = pltpu.get_barrier_semaphore()
    for where in (sibling, after, before):
        pl.semaphore_signal(barrier, inc=1, device_id=where, device_id_type=MESH)

    flat = jnp.concatenate([o_ref[h] for h in range(4)], axis=0).astype(jnp.float32)
    x[...] = jnp.transpose(flat).astype(jnp.bfloat16)
    pl.semaphore_wait(barrier, 3)

    a_rows, b_rows = slice(0, HALF), slice(HALF, ROWS)

    def product(key, rows):
        return jnp.dot(x[rows, :], wbuf[owner(*key)], preferred_element_type=jnp.float32)

    across = []

    def give(i):
        loads[(order[i], 1)].wait()
        for rows in (a_rows, b_rows):
            sib_out[i, rows, :] = product((order[i], 1), rows).astype(jnp.bfloat16)
        copy = remote(sib_out.at[i], sib_in.at[i], sib_send.at[i], sib_recv.at[i], sibling)
        copy.start()
        across.append(copy)

    def own(i, rows):
        return product((order[i], 0), rows) + sib_in[i, rows, :].astype(jnp.float32)

    def leave(i, rows, target):
        k = 2 * i + (0 if rows is a_rows else 1)
        copy = remote(tx.at[i, rows], rx.at[i, rows], send.at[k], recv.at[k], target)
        copy.start()
        return copy

    give(0)
    give(1)
    loads[(2, 0)].wait()
    across[0].wait_recv()
    tx[0, a_rows, :] = own(0, a_rows).astype(jnp.bfloat16)
    far_a = leave(0, a_rows, after)
    tx[0, b_rows, :] = own(0, b_rows).astype(jnp.bfloat16)
    far_b = leave(0, b_rows, before)
    give(2)
    loads[(1, 0)].wait()
    across[1].wait_recv()
    tx[1, b_rows, :] = own(1, b_rows).astype(jnp.bfloat16)
    next_b = leave(1, b_rows, after)
    loads[(3, 0)].wait()
    across[2].wait_recv()
    tx[2, a_rows, :] = own(2, a_rows).astype(jnp.bfloat16)
    prev_a = leave(2, a_rows, before)
    far_a.wait_recv()
    tx[1, a_rows, :] = (own(1, a_rows) + rx[0, a_rows, :].astype(jnp.float32)).astype(jnp.bfloat16)
    next_a = leave(1, a_rows, after)
    far_b.wait_recv()
    tx[2, b_rows, :] = (own(2, b_rows) + rx[0, b_rows, :].astype(jnp.float32)).astype(jnp.bfloat16)
    prev_b = leave(2, b_rows, before)
    give(3)
    loads[(0, 0)].wait()
    across[3].wait_recv()
    next_b.wait_recv()
    prev_a.wait_recv()
    next_a.wait_recv()
    prev_b.wait_recv()
    for rows in (a_rows, b_rows):
        whole = own(3, rows) + rx[1, rows, :].astype(jnp.float32) + rx[2, rows, :].astype(jnp.float32)
        out_ref[rows, :] = whole.astype(jnp.bfloat16)
    for copy in across + [far_a, far_b, next_a, next_b, prev_a, prev_b]:
        copy.wait_send()


VMEM = pl.BlockSpec(memory_space=pltpu.VMEM)
ANY = pl.BlockSpec(memory_space=pl.ANY)
DMA = pltpu.SemaphoreType.DMA


def params(number):
    return pltpu.CompilerParams(
        collective_id=number, has_side_effects=True, vmem_limit_bytes=60 * 1024 * 1024
    )


def per_device(hidden_in, ln_gain, w_qkv, w_out, doc_lengths, segment_ids, pair_table, page_table):
    b = lax.axis_index("blk")
    bf16, f32 = jnp.bfloat16, jnp.float32
    starts = jnp.cumsum(doc_lengths) - doc_lengths
    tokens = jnp.arange(16 * ROWS, dtype=jnp.int32)
    low = jnp.max(jnp.where(starts[:, None] <= tokens[None, :], starts[:, None], 0), axis=0)
    low = low.reshape(16, 1, ROWS)
    mine = jnp.arange(ROWS, dtype=jnp.int32)
    positions = b * ROWS + mine - lax.dynamic_index_in_dim(low, b, 0, keepdims=False)[0]
    frequency = 10000.0 ** (-(2.0 * jnp.arange(ROT // 2, dtype=f32)) / ROT)
    angles = frequency[:, None] * positions.astype(f32)[None, :]
    cosine, sine = jnp.cos(angles), jnp.sin(angles)
    table = jnp.stack([jnp.concatenate([cosine, cosine]), jnp.concatenate([-sine, sine])])
    local_pages = page_table - b * (ROWS // PAGE)
    dest = (local_pages[:, None] * PAGE + jnp.arange(PAGE, dtype=jnp.int32)[None, :]).reshape(1, ROWS)

    qkv = pl.pallas_call(
        project_kernel,
        out_shape=jax.ShapeDtypeStruct((4, 3, HD, ROWS), bf16),
        in_specs=[VMEM, VMEM, VMEM, ANY],
        out_specs=VMEM,
        scratch_shapes=[
            pltpu.VMEM((8, ROWS, SHARD), bf16),
            pltpu.VMEM((3, 8 * SHARD, COLS), bf16),
            pltpu.VMEM((3, ROWS, COLS), f32),
            pltpu.VMEM((8, 8, ROWS), f32),
            pltpu.VMEM((2, ROWS, 128), f32),
            pltpu.VMEM((HALF, SHARD), bf16),
            DMA((8,)), DMA, DMA((7,)), DMA((7,)), DMA((6,)), DMA((6,)), DMA((7,)), DMA((7,)),
        ],
        compiler_params=params(0),
        name="project",
    )(hidden_in, ln_gain.reshape(8, 1, SHARD), table, jnp.transpose(w_qkv, (1, 0, 2)))

    heads, pages = pl.pallas_call(
        attend_kernel,
        out_shape=(
            jax.ShapeDtypeStruct((4, HD, ROWS), bf16),
            jax.ShapeDtypeStruct((2, ROWS, COLS), bf16),
        ),
        in_specs=[VMEM, VMEM, VMEM],
        out_specs=(VMEM, VMEM),
        scratch_shapes=[
            pltpu.VMEM((4, HD, ROWS), bf16),
            pltpu.VMEM((4, 4, 2, HD, ROWS), bf16),
            pltpu.VMEM((4, 4, ROWS, HD), bf16),
            pltpu.VMEM((1, ROWS), f32),
            pltpu.VMEM((1, ROWS), f32),
            pltpu.VMEM((HD, ROWS), f32),
            pltpu.VMEM((4, HD, ROWS), bf16),
            DMA((2,)), DMA((3,)), DMA((3,)), DMA((3,)), DMA((3,)),
            DMA((4, 3)), DMA((4, 3)), DMA((3,)), DMA((3,)),
        ],
        compiler_params=params(1),
        name="attend",
    )(qkv, low, dest)

    attn_out = pl.pallas_call(
        output_kernel,
        out_shape=jax.ShapeDtypeStruct((ROWS, SHARD), bf16),
        in_specs=[VMEM, ANY],
        out_specs=VMEM,
        scratch_shapes=[
            pltpu.VMEM((8, COLS, SHARD), bf16),
            pltpu.VMEM((ROWS, COLS), bf16),
            pltpu.VMEM((4, ROWS, SHARD), bf16),
            pltpu.VMEM((4, ROWS, SHARD), bf16),
            pltpu.VMEM((3, ROWS, SHARD), bf16),
            pltpu.VMEM((3, ROWS, SHARD), bf16),
            DMA((8,)), DMA((4,)), DMA((4,)), DMA((6,)), DMA((6,)),
        ],
        compiler_params=params(2),
        name="output",
    )(heads, w_out)
    return attn_out, pages.reshape(2, ROWS // PAGE, PAGE, COLS)


def solution(mesh):
    placed = (P("blk", "tp"), P(), P(None, None, "tp"), P("tp", None), P(), P("blk"), P(), P("blk"))
    return jax.shard_map(
        per_device,
        mesh=mesh,
        in_specs=placed,
        out_specs=(P("blk", "tp"), P(None, "blk", None, "tp")),
        check_vma=False,
    )
```

time: 352 us -> 141 us (0.40)
  the two profiles are of different devices: /device:TPU:1 before, /device:TPU:24 now
where the time goes in v1:
time: 141 us
  Pallas kernels  133 us (94%)
  local copies, waits for them, and re-layouts  4.46 us (3%)
  other arithmetic  2.91 us (2%)
    pallas_call x1, Pallas kernels, per_device(): pl.pallas_call(attend_kernel, out_shape=(jax.ShapeDtypeStruct((4, HD, ROW...  52.5 us
    pallas_call x1, Pallas kernels, per_device(): pl.pallas_call(project_kernel, out_shape=jax.ShapeDtypeStruct((4, 3, HD,...  41.3 us
    pallas_call x1, Pallas kernels, per_device(): pl.pallas_call(output_kernel, out_shape=jax.ShapeDtypeStruct((ROWS, SHARD...  38.7 us
    unnamed x6, local copies, waits for them, and re-layouts  3.03 us

profile of v1, /device:TPU:24, one launch (start us, length us, event | category | flops | bytes accessed | tf_op | source)
XLA Modules:
  0.0 140.6 jit_solution(6537931255839209161)
XLA Ops:
  0.6 0.7 subtract_multiply_fusion
  1.3 0.1 iota_add_fusion
  1.4 0.7 add.43.dest_ref
  2.1 0.7 copy.10
  2.8 0.1 reduce-window.9
  2.9 0.1 reduce
  3.0 0.7 sub.16
  3.7 0.4 select_reduce_fusion
  4.1 0.0 copy-start.1
  4.2 0.2 multiply_cosine_fusion
  4.4 0.6 pad_maximum_fusion.table_ref
  5.0 41.3 %project.1.qkv_ref = bf16[4,3,96,512]{3,2,1,0:T(8,128)(2,1)} custom-call(bf16[512,768]{1,0:T(8,128)(2,1)} %hid_ref.1, f32[8,1,768]{2,1,0:T(1,128)} %bitcast.14, f32[2,24,512]{2,1,0:T(8,128)} %pad_maximum_fusion.table_ref, bf16[3,6144,384]{2,1,0:T(8,128)(2,1)} %bitcast.10), custom_call_target="tpu_custom_call" | custom-call | tf_op jit(solution)/shard_map/project/pallas_call | solution.py:461
  46.4 0.0 copy-done.1
  46.4 52.5 %attend.1 = (bf16[4,96,512]{2,1,0:T(8,128)(2,1)}, bf16[2,512,384]{2,1,0:T(8,128)(2,1)}) custom-call(bf16[4,3,96,512]{3,2,1,0:T(8,128)(2,1)} %project.1.qkv_ref, s32[16,1,512]{2,1,0:T(1,128)} %bitcast.13, s32[1,512]{1,0:T(1,128)} %add.43.dest_ref), custom_call_target="tpu_custom_call" | custom-call | tf_op jit(solution)/shard_map/attend/pallas_call | solution.py:479
  98.9 38.7 %output.1 = bf16[512,768]{1,0:T(8,128)(2,1)} custom-call(bf16[4,96,512]{2,1,0:T(8,128)(2,1)} %get-tuple-element.4.o_ref, bf16[384,6144]{1,0:T(8,128)(2,1)} %w_ref.1), custom_call_target="tpu_custom_call" | custom-call | tf_op jit(solution)/shard_map/output/pallas_call | solution.py:502
  137.6 0.0 copy-start
  137.6 2.1 %copy.13 = bf16[512,768]{1,0:T(8,128)(2,1)} copy(bf16[512,768]{1,0:T(8,128)(2,1)} %output.1) | data formatting | bytes 1572864
  139.7 0.0 copy-done
  139.7 0.9 copy.14
  (4 shorter events, 0.0 us)
Async XLA Ops:
  4.1 42.3 %copy-start.1 = (s32[8192]{0:T(1024)}, s32[8192]{0:T(1024)S(1)}, u32[]{:S(2)}) copy-start(s32[8192]{0:T(1024)S(1)} %select_reduce_fusion) | copy-start | bytes 98308
  137.6 2.1 %copy-start = (bf16[2,512,384]{2,1,0:T(8,128)(2,1)S(1)}, bf16[2,512,384]{2,1,0:T(8,128)(2,1)}, u32[]{:S(2)}) copy-start(bf16[2,512,384]{2,1,0:T(8,128)(2,1)} %get-tuple-element.5) | copy-start | bytes 2359300

commit v2 on v0

v2 whole, which is shorter than its diff:
```python
import jax
import jax.numpy as jnp
import numpy as np
from jax import lax
from jax.experimental import pallas as pl
from jax.experimental.pallas import tpu as pltpu
from jax.sharding import PartitionSpec as P

HD = 96
ROT = 24
PAGE = 16
ROWS = 512
HALF = 256
QUARTER = 128
SHARD = 768
COLS = 384
EPSILON = 1e-05
FACTOR = 1.4426950408889634 * HD ** (-0.5)
LOWEST = -1e30
MESH = pl.DeviceIdType.MESH
F32, BF16 = jnp.float32, jnp.bfloat16


def remote(src, dst, send, recv, where):
    return pltpu.make_async_remote_copy(
        src_ref=src, dst_ref=dst, send_sem=send, recv_sem=recv, device_id=where, device_id_type=MESH
    )


def iota(shape, axis):
    return lax.broadcasted_iota(jnp.int32, shape, axis)


def layer_kernel(
    hid_ref, gain_ref, lens_ref, pages_ref, freq_ref, wqkv_ref, wout_ref,
    out_ref, page_ref,
    gathered, wbuf, acc, stats, columns, normed, table, qkv, qbuf, kv, keys, lows,
    peak, total, mix, done, heads, wo, x, sib_out, sib_in, tx, rx, hold, far_hold,
    w_sem, wo_sem, own_sem, stat_send, stat_recv, ici_send, ici_recv, sib_send, sib_recv,
    keep_sem, kv_send, kv_recv, q_send, q_recv, ag_send, ag_recv, o_send, o_recv,
    give_send, give_recv, ring_send, ring_recv,
):
    b = lax.axis_index("blk")
    t = lax.axis_index("tp")
    z, c = t // 2, t % 2
    y, xx = b // 4, b % 4
    sibling = (b, z * 2 + 1 - c)
    after = (b, ((z + 1) % 4) * 2 + c)
    before = (b, ((z + 3) % 4) * 2 + c)
    mine = (1 - c) * y + c * xx
    group = (1 - c) * xx + c * y
    order = (1, 3, 2)

    def block_of(a, g):
        return (1 - c) * (a * 4 + g) + c * (g * 4 + a)

    def origin(dz, k):
        return ((z + dz) % 4) * 2 + (c + k) % 2

    shard_order = [(0, 0), (0, 1), (3, 0), (1, 0), (3, 1), (1, 1), (2, 0), (2, 1)]
    loads = {}
    for i, key in enumerate(shard_order):
        rows = pl.ds(pl.multiple_of(origin(*key) * SHARD, SHARD), SHARD)
        loads[key] = pltpu.make_async_copy(wqkv_ref.at[:, rows, :], wbuf.at[:, rows, :], w_sem.at[i])
        loads[key].start()
    own_copy = pltpu.make_async_copy(hid_ref, gathered.at[t], own_sem)
    own_copy.start()
    out_loads = {}
    for i, key in enumerate([(2, 1), (2, 0), (1, 1), (1, 0), (3, 1), (3, 0), (0, 1), (0, 0)]):
        who = origin(*key)
        span = pl.ds(pl.multiple_of(who * SHARD, SHARD), SHARD)
        out_loads[key] = pltpu.make_async_copy(wout_ref.at[:, span], wo.at[who], wo_sem.at[i])
        out_loads[key].start()

    barrier = pltpu.get_barrier_semaphore()
    for d in range(1, 8):
        pl.semaphore_signal(barrier, inc=1, device_id=(b, (t + d) % 8), device_id_type=MESH)
    for d in range(1, 4):
        for where in (block_of((mine + d) % 4, group), block_of(mine, (group + d) % 4)):
            pl.semaphore_signal(barrier, inc=1, device_id=(where, t), device_id_type=MESH)

    value = hid_ref[...].astype(F32)
    mean = jnp.sum(value, axis=1, keepdims=True) * (1.0 / SHARD)
    centred = value - mean
    spread = jnp.sum(centred * centred, axis=1, keepdims=True)
    stats[t] = jnp.transpose(jnp.where(iota((ROWS, 128), 1) == 0, mean, spread))[:8]
    pl.semaphore_wait(barrier, 13)

    stat_copies = []
    for d in range(1, 8):
        copy = remote(stats.at[t], stats.at[t], stat_send.at[d - 1], stat_recv.at[d - 1], (b, (t + d) % 8))
        copy.start()
        stat_copies.append(copy)

    def part(half, k):
        return pl.ds(half * HALF + k * QUARTER, QUARTER)

    plus, minus, across = [], [], []
    for half in range(2):
        q0, q1 = part(half, 0), part(half, 1)
        both = pl.ds(half * HALF, HALF)
        left, right, far = origin(3, 0), origin(1, 0), origin(2, 0)

        def ici(i, who, rows, src, where):
            return remote(src.at[rows], gathered.at[who, rows], ici_send.at[half, i], ici_recv.at[half, i], where)

        plus.append([
            ici(0, t, q0, hid_ref, after), ici(1, t, q1, hid_ref, after), ici(2, left, q0, gathered.at[left], after),
        ])
        minus.append([
            ici(3, t, q1, hid_ref, before), ici(4, t, q0, hid_ref, before), ici(5, right, q1, gathered.at[right], before),
        ])
        moved = [(t, both), (left, q0), (right, q1), (left, q1), (right, q0), (far, q0), (far, q1)]
        across.append([
            remote(
                (hid_ref if i == 0 else gathered.at[who]).at[rows], gathered.at[who, rows],
                sib_send.at[half, i], sib_recv.at[half, i], sibling,
            )
            for i, (who, rows) in enumerate(moved)
        ])

    def send_own(half):
        plus[half][0].start()
        minus[half][0].start()
        across[half][0].start()
        plus[half][1].start()
        minus[half][1].start()

    send_own(0)

    lens = lens_ref[...].astype(F32)
    earlier = iota((64, 64), 1) < iota((64, 64), 0)
    starts = jnp.sum(jnp.where(earlier, lens, 0.0), axis=1, keepdims=True)

    def lowest(block, half):
        token = (block * ROWS + half * HALF + iota((1, HALF), 1)).astype(F32)
        return token, jnp.max(jnp.where(starts <= token, starts, 0.0), axis=0, keepdims=True)

    for half in range(2):
        token, low = lowest(b, half)
        angle = freq_ref[:, 0:1] * (token - low)
        table[half, 0] = jnp.cos(angle)
        table[half, 1] = jnp.where(iota((ROT, HALF), 0) < ROT // 2, -1.0, 1.0) * jnp.sin(angle)
        for slot in range(4):
            lows[half, slot] = lowest(block_of(slot, group), half)[1]

    for copy in stat_copies:
        copy.wait_recv()
    means = stats[:, 0, :]
    whole_mean = jnp.sum(means, axis=0, keepdims=True) * 0.125
    off = means - whole_mean
    squares = jnp.sum(stats[:, 1, :], axis=0, keepdims=True) + SHARD * jnp.sum(off * off, axis=0, keepdims=True)
    inverse = lax.rsqrt(squares * (1.0 / (8 * SHARD)) + EPSILON)
    columns[0] = jnp.transpose(jnp.broadcast_to(whole_mean, (128, ROWS)))
    columns[1] = jnp.transpose(jnp.broadcast_to(inverse, (128, ROWS)))

    def compute(key, half):
        who = origin(*key)

        def normalise(i, carry):
            rows = pl.ds(pl.multiple_of(half * HALF + i * 64, 64), 64)
            here = pl.ds(pl.multiple_of(i * 64, 64), 64)
            centre, scale = columns[0, rows, :], columns[1, rows, :]
            for j in range(SHARD // 128):
                span = slice(128 * j, 128 * j + 128)
                normed[here, span] = (
                    (gathered[who, rows, span].astype(F32) - centre) * scale * gain_ref[who, :, span]
                ).astype(BF16)
            return carry

        lax.fori_loop(0, HALF // 64, normalise, 0)
        depth = pl.ds(pl.multiple_of(who * SHARD, SHARD), SHARD)
        fresh = key == (0, 0)

        def multiply(kind, carry):
            product = jnp.dot(normed[...], wbuf[kind, depth, :], preferred_element_type=F32)
            if fresh:
                acc[kind] = product
            else:
                acc[kind] += product
            return carry

        lax.fori_loop(0, 3, multiply, 0)

    def epilogue(half):
        cosine, sine = table[half, 0], table[half, 1]
        for kind in range(3):
            turned = jnp.transpose(acc[kind])
            for h in range(COLS // HD):
                piece = turned[h * HD:(h + 1) * HD]
                if kind < 2:
                    top = piece[:ROT]
                    swapped = jnp.concatenate([top[ROT // 2:], top[:ROT // 2]], axis=0)
                    piece = jnp.concatenate([top * cosine + swapped * sine, piece[ROT:]], axis=0)
                qkv[half, h, kind] = piece.astype(BF16)

    pair = pl.ds(1, 2)
    kept, kv_copies, q_copies, ag_copies = [[], []], [[], []], [[], []], [[], []]

    def redistribute(half):
        copy = pltpu.make_async_copy(qkv.at[half, mine, pair], kv.at[half, group, mine], keep_sem.at[half, 0])
        copy.start()
        kept[half].append(copy)
        copy = pltpu.make_async_copy(qkv.at[half, mine, 0], qbuf.at[half, mine], keep_sem.at[half, 1])
        copy.start()
        kept[half].append(copy)
        for d in order:
            head = (mine + d) % 4
            copy = remote(
                qkv.at[half, head, pair], kv.at[half, group, mine],
                kv_send.at[half, d - 1], kv_recv.at[half, d - 1], (block_of(head, group), t),
            )
            copy.start()
            kv_copies[half].append(copy)
        for d in order:
            copy = remote(
                qkv.at[half, mine, pair], kv.at[half, group, mine],
                ag_send.at[half, 0, d - 1], ag_recv.at[half, 0, d - 1], (block_of(mine, (group + d) % 4), t),
            )
            copy.start()
            ag_copies[half].append(copy)
        for d in order:
            head = (mine + d) % 4
            copy = remote(
                qkv.at[half, head, 0], qbuf.at[half, mine],
                q_send.at[half, d - 1], q_recv.at[half, d - 1], (block_of(head, group), t),
            )
            copy.start()
            q_copies[half].append(copy)

    def relay(half, i):
        d = order[i]
        kv_copies[half][i].wait_recv()
        slot = (mine + 4 - d) % 4
        for e in order:
            copy = remote(
                kv.at[half, group, slot], kv.at[half, group, slot],
                ag_send.at[half, d, e - 1], ag_recv.at[half, d, e - 1], (block_of(mine, (group + e) % 4), t),
            )
            copy.start()
            ag_copies[half].append(copy)

    def relay_ring(half):
        plus[half][0].wait_recv()
        plus[half][2].start()
        across[half][1].start()
        minus[half][0].wait_recv()
        minus[half][2].start()
        across[half][2].start()

    own_copy.wait()
    for half in range(2):
        if half == 0:
            loads[(0, 0)].wait()
        compute((0, 0), half)
        relay_ring(half)
        if half == 0:
            send_own(1)
            loads[(0, 1)].wait()
        across[half][0].wait_recv()
        compute((0, 1), half)
        if half == 1:
            relay(0, 0)
        plus[half][1].wait_recv()
        across[half][3].start()
        minus[half][1].wait_recv()
        across[half][4].start()
        if half == 0:
            loads[(3, 0)].wait()
        compute((3, 0), half)
        if half == 1:
            relay(0, 1)
        if half == 0:
            loads[(1, 0)].wait()
        compute((1, 0), half)
        if half == 1:
            relay(0, 2)
        across[half][1].wait_recv()
        across[half][3].wait_recv()
        if half == 0:
            loads[(3, 1)].wait()
        compute((3, 1), half)
        across[half][2].wait_recv()
        across[half][4].wait_recv()
        if half == 0:
            loads[(1, 1)].wait()
        compute((1, 1), half)
        plus[half][2].wait_recv()
        across[half][5].start()
        minus[half][2].wait_recv()
        across[half][6].start()
        if half == 0:
            loads[(2, 0)].wait()
        compute((2, 0), half)
        across[half][5].wait_recv()
        across[half][6].wait_recv()
        if half == 0:
            loads[(2, 1)].wait()
        compute((2, 1), half)
        epilogue(half)
        redistribute(half)

    depth_index = iota((HALF, HALF), 0).astype(F32)
    query_index = iota((HALF, HALF), 1).astype(F32)

    def turn(half):
        def one(i, carry):
            keys[half, i // 4, i % 4] = jnp.transpose(kv[half, i // 4, i % 4, 0].astype(F32)).astype(BF16)
            return carry

        lax.fori_loop(0, 16, one, 0)

    def tile(slot, q_half, k_half, back, first, diagonal):
        key_block = block_of(slot, group) - back
        safe = (key_block + 16) % 16
        a = (1 - c) * (safe // 4) + c * (safe % 4)
        g = (1 - c) * (safe % 4) + c * (safe // 4)
        score = jnp.dot(keys[k_half, g, a], qbuf[q_half, slot], preferred_element_type=F32)
        base = (key_block * ROWS + k_half * HALF).astype(F32)
        allowed = depth_index >= lows[q_half, slot] - base
        if diagonal:
            allowed = allowed & (depth_index <= query_index)
        score = jnp.where(allowed, score, LOWEST)
        highest = jnp.max(score, axis=0, keepdims=True)
        if not first:
            previous = peak[q_half, slot]
            highest = jnp.maximum(highest, previous)
        weight = jnp.exp2((score - highest) * FACTOR)
        added = jnp.sum(weight, axis=0, keepdims=True)
        mixed = jnp.dot(kv[k_half, g, a, 1], weight.astype(BF16), preferred_element_type=F32)
        if first:
            total[q_half, slot] = added
            mix[q_half, slot] = mixed
        else:
            fade = jnp.exp2((previous - highest) * FACTOR)
            total[q_half, slot] = total[q_half, slot] * fade + added
            mix[q_half, slot] = mix[q_half, slot] * fade + mixed
        peak[q_half, slot] = highest

    def sweep(q_half, k_half, low, high):
        def one(back, carry):
            for slot in range(4):
                tile(slot, q_half, k_half, back, False, False)
            return carry

        lax.fori_loop(low, high, one, 0)

    def opening(q_half, k_half):
        for slot in range(4):
            tile(slot, q_half, k_half, 0, k_half == 0, q_half == k_half)

    o_copies = [[], []]

    def give_back(half):
        def one(slot, carry):
            done[half, slot] = (mix[half, slot] / total[half, slot]).astype(BF16)
            return carry

        lax.fori_loop(0, 4, one, 0)
        for d in order:
            slot = (mine + d) % 4
            copy = remote(
                done.at[half, slot], heads.at[half, mine],
                o_send.at[half, d - 1], o_recv.at[half, d - 1], (block_of(slot, group), t),
            )
            copy.start()
            o_copies[half].append(copy)
        heads[half, mine] = done[half, mine]

    for copy in kept[0]:
        copy.wait()
    for copy in q_copies[0] + ag_copies[0]:
        copy.wait_recv()
    turn(0)
    opening(0, 0)
    sweep(0, 0, 1, 4)
    relay(1, 0)
    relay(1, 1)
    relay(1, 2)
    sweep(0, 0, 4, 9)
    for copy in kept[1]:
        copy.wait()
    for copy in q_copies[1]:
        copy.wait_recv()
    opening(1, 0)
    sweep(1, 0, 1, 8)

    page_col = jnp.sum(
        jnp.where(iota((32, 32), 0) == iota((32, 32), 1), pages_ref[...].astype(F32), 0.0), axis=1, keepdims=True
    )
    spread_pages = jnp.where(iota((32, ROWS), 0) == iota((32, ROWS), 1) // PAGE, page_col, 0.0)
    shift = (iota((1, ROWS), 1) % PAGE - b * ROWS).astype(F32)
    target = jnp.sum(spread_pages, axis=0, keepdims=True) * PAGE + shift
    chosen = (iota((ROWS, ROWS), 0).astype(F32) == target).astype(F32).astype(BF16)
    for kind in range(2):
        moved = None
        for half in range(2):
            source = jnp.concatenate([qkv[half, h, kind + 1] for h in range(4)], axis=0)
            term = lax.dot_general(
                chosen[:, half * HALF:(half + 1) * HALF], source, (((1,), (1,)), ((), ())),
                preferred_element_type=F32,
            )
            moved = term if moved is None else moved + term
        page_ref[kind] = moved.astype(BF16).reshape(ROWS // PAGE, PAGE, COLS)

    for copy in ag_copies[1]:
        copy.wait_recv()
    turn(1)
    sweep(0, 1, 1, 9)
    give_back(0)

    rs_order = (2, 1, 3, 0)
    ring, across_sums = [{}, {}], [[], []]

    def product(half, key):
        return jnp.dot(x[half], wo[origin(*key)], preferred_element_type=F32)

    def leave(half, i, k, where):
        rows = pl.ds(k * QUARTER, QUARTER)
        n = 2 * i + k
        copy = remote(tx.at[half, i, rows], rx.at[half, i, rows], ring_send.at[half, n], ring_recv.at[half, n], where)
        copy.start()
        ring[half][(i, k)] = copy

    def first_part(half):
        for copy in o_copies[half]:
            copy.wait_recv()
        flat = jnp.concatenate([heads[half, h] for h in range(4)], axis=0).astype(F32)
        x[half] = jnp.transpose(flat).astype(BF16)

        def give(i):
            if half == 0:
                out_loads[(rs_order[i], 1)].wait()
            sib_out[half, i] = product(half, (rs_order[i], 1)).astype(BF16)
            copy = remote(sib_out.at[half, i], sib_in.at[half, i], give_send.at[half, i], give_recv.at[half, i], sibling)
            copy.start()
            across_sums[half].append(copy)

        def own(i):
            if half == 0:
                out_loads[(rs_order[i], 0)].wait()
            value = product(half, (rs_order[i], 0))
            across_sums[half][i].wait_recv()
            return value + sib_in[half, i].astype(F32)

        give(0)
        give(1)
        tx[half, 0] = own(0).astype(BF16)
        leave(half, 0, 0, after)
        leave(half, 0, 1, before)
        give(2)
        value = own(1)
        tx[half, 1, QUARTER:] = value[QUARTER:].astype(BF16)
        leave(half, 1, 1, after)
        hold[half, 0] = value[:QUARTER]
        give(3)
        value = own(2)
        tx[half, 2, :QUARTER] = value[:QUARTER].astype(BF16)
        leave(half, 2, 0, before)
        hold[half, 1] = value[QUARTER:]
        far_hold[half] = own(3)

    def second_part(half):
        ring[half][(0, 0)].wait_recv()
        tx[half, 1, :QUARTER] = (hold[half, 0] + rx[half, 0, :QUARTER].astype(F32)).astype(BF16)
        leave(half, 1, 0, after)
        ring[half][(0, 1)].wait_recv()
        tx[half, 2, QUARTER:] = (hold[half, 1] + rx[half, 0, QUARTER:].astype(F32)).astype(BF16)
        leave(half, 2, 1, before)

    def last_part(half):
        for key in ((1, 1), (2, 0), (1, 0), (2, 1)):
            ring[half][key].wait_recv()
        out_ref[half * HALF:(half + 1) * HALF, :] = (
            far_hold[half] + rx[half, 1].astype(F32) + rx[half, 2].astype(F32)
        ).astype(BF16)

    opening(1, 1)
    sweep(1, 1, 1, 4)
    first_part(0)
    sweep(1, 1, 4, 9)
    give_back(1)
    second_part(0)
    first_part(1)
    last_part(0)
    second_part(1)
    last_part(1)

    for copy in stat_copies:
        copy.wait_send()
    for half in range(2):
        for copy in plus[half] + minus[half] + across[half]:
            copy.wait_send()
        for copy in kv_copies[half] + q_copies[half] + ag_copies[half] + o_copies[half]:
            copy.wait_send()
        for copy in across_sums[half] + list(ring[half].values()):
            copy.wait_send()


VMEM = pl.BlockSpec(memory_space=pltpu.VMEM)
ANY = pl.BlockSpec(memory_space=pl.ANY)
DMA = pltpu.SemaphoreType.DMA


def per_device(hidden_in, ln_gain, w_qkv, w_out, doc_lengths, segment_ids, pair_table, page_table):
    frequency = 10000.0 ** (-(2.0 * (np.arange(ROT) % (ROT // 2))) / ROT)
    frequency = jnp.asarray(np.repeat(frequency[:, None], 128, axis=1), F32)
    scratch = [
        pltpu.VMEM((8, ROWS, SHARD), BF16),
        pltpu.VMEM((3, 8 * SHARD, COLS), BF16),
        pltpu.VMEM((3, HALF, COLS), F32),
        pltpu.VMEM((8, 8, ROWS), F32),
        pltpu.VMEM((2, ROWS, 128), F32),
        pltpu.VMEM((HALF, SHARD), BF16),
        pltpu.VMEM((2, 2, ROT, HALF), F32),
        pltpu.VMEM((2, 4, 3, HD, HALF), BF16),
        pltpu.VMEM((2, 4, HD, HALF), BF16),
        pltpu.VMEM((2, 4, 4, 2, HD, HALF), BF16),
        pltpu.VMEM((2, 4, 4, HALF, HD), BF16),
        pltpu.VMEM((2, 4, 1, HALF), F32),
        pltpu.VMEM((2, 4, 1, HALF), F32),
        pltpu.VMEM((2, 4, 1, HALF), F32),
        pltpu.VMEM((2, 4, HD, HALF), F32),
        pltpu.VMEM((2, 4, HD, HALF), BF16),
        pltpu.VMEM((2, 4, HD, HALF), BF16),
        pltpu.VMEM((8, COLS, SHARD), BF16),
        pltpu.VMEM((2, HALF, COLS), BF16),
        pltpu.VMEM((2, 4, HALF, SHARD), BF16),
        pltpu.VMEM((2, 4, HALF, SHARD), BF16),
        pltpu.VMEM((2, 3, HALF, SHARD), BF16),
        pltpu.VMEM((2, 3, HALF, SHARD), BF16),
        pltpu.VMEM((2, 2, QUARTER, SHARD), F32),
        pltpu.VMEM((2, HALF, SHARD), F32),
        DMA((8,)), DMA((8,)), DMA, DMA((7,)), DMA((7,)), DMA((2, 6)), DMA((2, 6)), DMA((2, 7)), DMA((2, 7)),
        DMA((2, 2)), DMA((2, 3)), DMA((2, 3)), DMA((2, 3)), DMA((2, 3)), DMA((2, 4, 3)), DMA((2, 4, 3)),
        DMA((2, 3)), DMA((2, 3)), DMA((2, 4)), DMA((2, 4)), DMA((2, 6)), DMA((2, 6)),
    ]
    attn_out, pages = pl.pallas_call(
        layer_kernel,
        out_shape=(
            jax.ShapeDtypeStruct((ROWS, SHARD), BF16),
            jax.ShapeDtypeStruct((2, ROWS // PAGE, PAGE, COLS), BF16),
        ),
        in_specs=[VMEM] * 5 + [ANY] * 2,
        out_specs=(VMEM, VMEM),
        scratch_shapes=scratch,
        compiler_params=pltpu.CompilerParams(
            collective_id=0, has_side_effects=True, vmem_limit_bytes=62 * 1024 * 1024
        ),
        name="layer",
    )(
        hidden_in, ln_gain.reshape(8, 1, SHARD), doc_lengths.reshape(1, 64), page_table.reshape(1, 32), frequency,
        jnp.transpose(w_qkv, (1, 0, 2)), w_out,
    )
    return attn_out, pages


def solution(mesh):
    placed = (P("blk", "tp"), P(), P(None, None, "tp"), P("tp", None), P(), P("blk"), P(), P("blk"))
    return jax.shard_map(
        per_device,
        mesh=mesh,
        in_specs=placed,
        out_specs=(P("blk", "tp"), P(None, "blk", None, "tp")),
        check_vma=False,
    )
```

time: 352 us -> 127 us (0.36)
  waiting for transfers between devices: 178 us -> 0 us
  Pallas kernels: 0 us -> 122 us
  matrix products: 75.9 us -> 0 us
  other arithmetic: 39.4 us -> 0 us
  local copies, waits for them, and re-layouts: 23.8 us -> 4.15 us
  blocking collectives: 19.2 us -> 0 us
  between operations: 14.7 us -> 0.64 us
    all_gather x3 -> x0, waiting for transfers between devices: 139 us -> none  [the longest x1 68.3 us: per_device(): value_piece = lax.all_gather(values, 'blk', axis=0, tiled=True)]
    pallas_call x0 -> x1, Pallas kernels: none -> 122 us  [per_device(): pl.pallas_call(layer_kernel, out_shape=(jax.ShapeDtypeStruct((ROWS, SHARD...]
    dot_general x4 -> x0, matrix products: 75.9 us -> none  [the longest x1 28.2 us: compute(): jnp.einsum('qhd,khd->hqk', queries, key_piece, preferred_element_type=jnp...]
    reduce_scatter x1 -> x0, waiting for transfers between devices: 38.9 us -> none  [per_device(): lax.psum_scatter(partial_term.astype(jnp.bfloat16), 'tp', scatter_dimensi...]
    reduce_sum x5 -> x0, other arithmetic: 31.4 us -> none  [the longest x1 22.7 us: compute(): totals = jnp.sum(weights, axis=-1)]
    all_gather x1 -> x0, blocking collectives: 19.2 us -> none  [per_device(): segment_piece = lax.all_gather(segment_ids, 'blk', axis=0, tiled=True)]
    unnamed x21 -> x2, local copies, waits for them, and re-layouts: 18.9 us -> 4.15 us
    and x1 -> x0, other arithmetic: 5.82 us -> none  [compute(): live[None, :] & (segment_ids[:, None] == segment_piece[None, :])]
  transfers between devices with their start and end apart: 4 -> 0, of which waited for: 4 -> 0; matrix products, arithmetic and copies ran while one was open for 7% -> 0% of each run, Pallas kernels for 0% -> 0%
where the time goes in v2:
time: 127 us
  Pallas kernels  122 us (96%)
  local copies, waits for them, and re-layouts  4.15 us (3%)
    pallas_call x1, Pallas kernels, per_device(): pl.pallas_call(layer_kernel, out_shape=(jax.ShapeDtypeStruct((ROWS, SHARD...  122 us
    unnamed x2, local copies, waits for them, and re-layouts  4.15 us

profile of v2, /device:TPU:1, one launch (start us, length us, event | category | flops | bytes accessed | tf_op | source)
XLA Modules:
  0.0 127.1 jit_solution(10841824052165085981)
XLA Ops:
  0.6 122.3 %layer.1 = (bf16[512,768]{1,0:T(8,128)(2,1)}, bf16[2,32,16,384]{3,2,1,0:T(8,128)(2,1)}) custom-call(bf16[512,768]{1,0:T(8,128)(2,1)} %hid_ref.1, f32[8,1,768]{2,1,0:T(1,128)} %bitcast.5, s32[1,64]{1,0:T(1,128)} %bitcast.6, s32[1,32]{1,0:T(1,128)} %bitcast.7, f32[24,128]{1,0:T(8,128)} %constant.2.clone.freq_ref, bf16[3,6144,384]{2,1,0:T(8,128)(2,1)} %bitcast.4, ...), custom_call_target="tpu_custom_call" | custom-call | tf_op jit(solution)/shard_map/layer/pallas_call | solution.py:538
  123.0 2.1 %copy.11 = bf16[512,768]{1,0:T(8,128)(2,1)} copy(bf16[512,768]{1,0:T(8,128)(2,1)} %get-tuple-element.4) | data formatting | bytes 1572864
  125.0 2.1 %copy.12 = bf16[2,32,16,384]{3,2,1,0:T(8,128)(2,1)} copy(bf16[2,32,16,384]{3,2,1,0:T(8,128)(2,1)} %get-tuple-element.5) | data formatting | bytes 1572864

commit v3 on v2

--- a/solution.py
+++ b/solution.py
@@ -35,7 +35,7 @@
     hid_ref, gain_ref, lens_ref, pages_ref, freq_ref, wqkv_ref, wout_ref,
     out_ref, page_ref,
     gathered, wbuf, acc, stats, columns, normed, table, qkv, qbuf, kv, keys, lows,
-    peak, total, mix, done, heads, wo, x, sib_out, sib_in, tx, rx, hold, far_hold,
+    scores, peak, total, mix, done, heads, wo, x, sib_in, rx, hold, far_hold,
     w_sem, wo_sem, own_sem, stat_send, stat_recv, ici_send, ici_recv, sib_send, sib_recv,
     keep_sem, kv_send, kv_recv, q_send, q_recv, ag_send, ag_recv, o_send, o_recv,
     give_send, give_recv, ring_send, ring_recv,
@@ -310,44 +310,58 @@
 
         lax.fori_loop(0, 16, one, 0)
 
-    def tile(slot, q_half, k_half, back, first, diagonal):
-        key_block = block_of(slot, group) - back
-        safe = (key_block + 16) % 16
-        a = (1 - c) * (safe // 4) + c * (safe % 4)
-        g = (1 - c) * (safe % 4) + c * (safe // 4)
-        score = jnp.dot(keys[k_half, g, a], qbuf[q_half, slot], preferred_element_type=F32)
-        base = (key_block * ROWS + k_half * HALF).astype(F32)
-        allowed = depth_index >= lows[q_half, slot] - base
-        if diagonal:
-            allowed = allowed & (depth_index <= query_index)
-        score = jnp.where(allowed, score, LOWEST)
-        highest = jnp.max(score, axis=0, keepdims=True)
+    def unit(slot, q_half, k_half, backs, first):
+        query_block = block_of(slot, group)
+        low, query = lows[q_half, slot], qbuf[q_half, slot]
+
+        def place(back):
+            key_block = query_block - back
+            safe = (key_block + 16) % 16
+            return key_block, (1 - c) * (safe // 4) + c * (safe % 4), (1 - c) * (safe % 4) + c * (safe // 4)
+
+        rough = None
+        for i, back in enumerate(backs):
+            key_block, a, g = place(back)
+            score = jnp.dot(keys[k_half, g, a], query, preferred_element_type=F32)
+            allowed = depth_index >= low - (key_block * ROWS + k_half * HALF).astype(F32)
+            if back == 0 and q_half == k_half:
+                allowed = allowed & (depth_index <= query_index)
+            score = jnp.where(allowed, score, LOWEST)
+            scores[i] = score
+            tallest = jnp.max(score.reshape(HALF // 8, 8, HALF), axis=0)
+            rough = tallest if rough is None else jnp.maximum(rough, tallest)
+        highest = jnp.max(rough, axis=0, keepdims=True)
         if not first:
             previous = peak[q_half, slot]
             highest = jnp.maximum(highest, previous)
-        weight = jnp.exp2((score - highest) * FACTOR)
-        added = jnp.sum(weight, axis=0, keepdims=True)
-        mixed = jnp.dot(kv[k_half, g, a, 1], weight.astype(BF16), preferred_element_type=F32)
+            fade = jnp.exp2((previous - highest) * FACTOR)
+        sums, mixed = None, None
+        for i, back in enumerate(backs):
+            _, a, g = place(back)
+            weight = jnp.exp2((scores[i] - highest) * FACTOR)
+            added = jnp.sum(weight.reshape(HALF // 8, 8, HALF), axis=0)
+            term = jnp.dot(kv[k_half, g, a, 1], weight.astype(BF16), preferred_element_type=F32)
+            sums = added if sums is None else sums + added
+            mixed = term if mixed is None else mixed + term
+        added = jnp.sum(sums, axis=0, keepdims=True)
         if first:
             total[q_half, slot] = added
             mix[q_half, slot] = mixed
         else:
-            fade = jnp.exp2((previous - highest) * FACTOR)
             total[q_half, slot] = total[q_half, slot] * fade + added
             mix[q_half, slot] = mix[q_half, slot] * fade + mixed
         peak[q_half, slot] = highest
 
-    def sweep(q_half, k_half, low, high):
-        def one(back, carry):
-            for slot in range(4):
-                tile(slot, q_half, k_half, back, False, False)
+    def sweep(q_half, k_half, low_slot=0, high_slot=4):
+        newest = 0 if k_half <= q_half else 1
+        oldest = 9 if k_half >= q_half else 8
+        backs = list(range(newest, oldest))
+
+        def one(slot, carry):
+            unit(slot, q_half, k_half, backs, k_half == 0)
             return carry
 
-        lax.fori_loop(low, high, one, 0)
-
-    def opening(q_half, k_half):
-        for slot in range(4):
-            tile(slot, q_half, k_half, 0, k_half == 0, q_half == k_half)
+        lax.fori_loop(low_slot, high_slot, one, 0)
 
     o_copies = [[], []]
 
@@ -372,18 +386,16 @@
     for copy in q_copies[0] + ag_copies[0]:
         copy.wait_recv()
     turn(0)
-    opening(0, 0)
-    sweep(0, 0, 1, 4)
+    sweep(0, 0, 0, 2)
     relay(1, 0)
     relay(1, 1)
     relay(1, 2)
-    sweep(0, 0, 4, 9)
+    sweep(0, 0, 2, 4)
     for copy in kept[1]:
         copy.wait()
     for copy in q_copies[1]:
         copy.wait_recv()
-    opening(1, 0)
-    sweep(1, 0, 1, 8)
+    sweep(1, 0)
 
     page_col = jnp.sum(
         jnp.where(iota((32, 32), 0) == iota((32, 32), 1), pages_ref[...].astype(F32), 0.0), axis=1, keepdims=True
@@ -406,7 +418,7 @@
     for copy in ag_copies[1]:
         copy.wait_recv()
     turn(1)
-    sweep(0, 1, 1, 9)
+    sweep(0, 1)
     give_back(0)
 
     rs_order = (2, 1, 3, 0)
@@ -414,11 +426,14 @@
 
     def product(half, key):
         return jnp.dot(x[half], wo[origin(*key)], preferred_element_type=F32)
+
+    def tx(half, i, k):
+        return gathered.at[4 + i, part(half, k)]
 
     def leave(half, i, k, where):
         rows = pl.ds(k * QUARTER, QUARTER)
         n = 2 * i + k
-        copy = remote(tx.at[half, i, rows], rx.at[half, i, rows], ring_send.at[half, n], ring_recv.at[half, n], where)
+        copy = remote(tx(half, i, k), rx.at[half, i, rows], ring_send.at[half, n], ring_recv.at[half, n], where)
         copy.start()
         ring[half][(i, k)] = copy
 
@@ -431,8 +446,8 @@
         def give(i):
             if half == 0:
                 out_loads[(rs_order[i], 1)].wait()
-            sib_out[half, i] = product(half, (rs_order[i], 1)).astype(BF16)
-            copy = remote(sib_out.at[half, i], sib_in.at[half, i], give_send.at[half, i], give_recv.at[half, i], sibling)
+            gathered[i, pl.ds(half * HALF, HALF), :] = product(half, (rs_order[i], 1)).astype(BF16)
+            copy = remote(gathered.at[i, pl.ds(half * HALF, HALF)], sib_in.at[half, i], give_send.at[half, i], give_recv.at[half, i], sibling)
             copy.start()
             across_sums[half].append(copy)
 
@@ -445,27 +460,27 @@
 
         give(0)
         give(1)
-        tx[half, 0] = own(0).astype(BF16)
+        gathered[4, pl.ds(half * HALF, HALF), :] = own(0).astype(BF16)
         leave(half, 0, 0, after)
         leave(half, 0, 1, before)
         give(2)
         value = own(1)
-        tx[half, 1, QUARTER:] = value[QUARTER:].astype(BF16)
+        tx(half, 1, 1)[...] = value[QUARTER:].astype(BF16)
         leave(half, 1, 1, after)
         hold[half, 0] = value[:QUARTER]
         give(3)
         value = own(2)
-        tx[half, 2, :QUARTER] = value[:QUARTER].astype(BF16)
+        tx(half, 2, 0)[...] = value[:QUARTER].astype(BF16)
         leave(half, 2, 0, before)
         hold[half, 1] = value[QUARTER:]
         far_hold[half] = own(3)
 
     def second_part(half):
         ring[half][(0, 0)].wait_recv()
-        tx[half, 1, :QUARTER] = (hold[half, 0] + rx[half, 0, :QUARTER].astype(F32)).astype(BF16)
+        tx(half, 1, 0)[...] = (hold[half, 0] + rx[half, 0, :QUARTER].astype(F32)).astype(BF16)
         leave(half, 1, 0, after)
         ring[half][(0, 1)].wait_recv()
-        tx[half, 2, QUARTER:] = (hold[half, 1] + rx[half, 0, QUARTER:].astype(F32)).astype(BF16)
+        tx(half, 2, 1)[...] = (hold[half, 1] + rx[half, 0, QUARTER:].astype(F32)).astype(BF16)
         leave(half, 2, 1, before)
 
     def last_part(half):
@@ -475,10 +490,12 @@
             far_hold[half] + rx[half, 1].astype(F32) + rx[half, 2].astype(F32)
         ).astype(BF16)
 
-    opening(1, 1)
-    sweep(1, 1, 1, 4)
+    sweep(1, 1, 0, 2)
+    for half in range(2):
+        for copy in plus[half] + minus[half] + across[half]:
+            copy.wait_send()
     first_part(0)
-    sweep(1, 1, 4, 9)
+    sweep(1, 1, 2, 4)
     give_back(1)
     second_part(0)
     first_part(1)
@@ -489,8 +506,6 @@
     for copy in stat_copies:
         copy.wait_send()
     for half in range(2):
-        for copy in plus[half] + minus[half] + across[half]:
-            copy.wait_send()
         for copy in kv_copies[half] + q_copies[half] + ag_copies[half] + o_copies[half]:
             copy.wait_send()
         for copy in across_sums[half] + list(ring[half].values()):
@@ -518,6 +533,7 @@
         pltpu.VMEM((2, 4, 4, 2, HD, HALF), BF16),
         pltpu.VMEM((2, 4, 4, HALF, HD), BF16),
         pltpu.VMEM((2, 4, 1, HALF), F32),
+        pltpu.VMEM((9, HALF, HALF), F32),
         pltpu.VMEM((2, 4, 1, HALF), F32),
         pltpu.VMEM((2, 4, 1, HALF), F32),
         pltpu.VMEM((2, 4, HD, HALF), F32),
@@ -526,8 +542,6 @@
         pltpu.VMEM((8, COLS, SHARD), BF16),
         pltpu.VMEM((2, HALF, COLS), BF16),
         pltpu.VMEM((2, 4, HALF, SHARD), BF16),
-        pltpu.VMEM((2, 4, HALF, SHARD), BF16),
-        pltpu.VMEM((2, 3, HALF, SHARD), BF16),
         pltpu.VMEM((2, 3, HALF, SHARD), BF16),
         pltpu.VMEM((2, 2, QUARTER, SHARD), F32),
         pltpu.VMEM((2, HALF, SHARD), F32),
@@ -545,7 +559,7 @@
         out_specs=(VMEM, VMEM),
         scratch_shapes=scratch,
         compiler_params=pltpu.CompilerParams(
-            collective_id=0, has_side_effects=True, vmem_limit_bytes=62 * 1024 * 1024
+            collective_id=0, has_side_effects=True, vmem_limit_bytes=49 * 1024 * 1024
         ),
         name="layer",
     )(

time: 127 us -> 107 us (0.84)
  Pallas kernels: 122 us -> 100 us
  local copies, waits for them, and re-layouts: 4.15 us -> 5.64 us
    pallas_call x1, Pallas kernels: 122 us -> 100 us  [per_device(): pl.pallas_call(layer_kernel, out_shape=(jax.ShapeDtypeStruct((ROWS, SHARD...]
    unnamed x2 -> x12, local copies, waits for them, and re-layouts: 4.15 us -> 5.64 us
where the time goes in v3:
time: 107 us; the launch traced here: 106 us
  Pallas kernels  100 us (93%)
  local copies, waits for them, and re-layouts  5.64 us (5%)
    pallas_call x1, Pallas kernels, per_device(): pl.pallas_call(layer_kernel, out_shape=(jax.ShapeDtypeStruct((ROWS, SHARD...  100 us
    unnamed x12, local copies, waits for them, and re-layouts  5.64 us

profile of v3, /device:TPU:1, one launch (start us, length us, event | category | flops | bytes accessed | tf_op | source)
XLA Modules:
  0.0 106.4 jit_solution(1661269752373470543)
XLA Ops:
  0.6 0.0 copy-start
  0.6 1.1 %copy-done = bf16[512,768]{1,0:T(8,128)(2,1)S(1)} copy-done((bf16[512,768]{1,0:T(8,128)(2,1)S(1)}, bf16[512,768]{1,0:T(8,128)(2,1)}, u32[]{:S(2)}) %copy-start) | copy-done | bytes 786456
  1.8 0.0 copy-start.1
  1.8 0.7 copy-done.1
  2.5 0.0 copy-start.2
  2.5 0.7 copy-done.2
  3.2 0.0 copy-start.3
  3.2 0.7 copy-done.3
  3.9 0.0 copy-start.4
  3.9 0.7 copy-done.4
  4.5 100.1 %layer.1 = (bf16[512,768]{1,0:T(8,128)(2,1)S(1)}, bf16[2,32,16,384]{3,2,1,0:T(8,128)(2,1)S(1)}) custom-call(bf16[512,768]{1,0:T(8,128)(2,1)S(1)} %copy-done, f32[8,1,768]{2,1,0:T(1,128)S(1)} %bitcast.4, s32[1,64]{1,0:T(1,128)S(1)} %bitcast.5, s32[1,32]{1,0:T(1,128)S(1)} %bitcast.6, f32[24,128]{1,0:T(8,128)S(1)} %copy-done.2, bf16[3,6144,384]{2,1,0:T(8,128)(2,1)} %bitcast.7, ...), custom_call_target="tpu_custom_call" | custom-call | tf_op jit(solution)/shard_map/layer/pallas_call | solution.py:552
  104.6 0.9 copy.11
  105.5 0.9 copy.12
Async XLA Ops:
  0.6 1.1 %copy-start = (bf16[512,768]{1,0:T(8,128)(2,1)S(1)}, bf16[512,768]{1,0:T(8,128)(2,1)}, u32[]{:S(2)}) copy-start(bf16[512,768]{1,0:T(8,128)(2,1)} %hid_ref.1) | copy-start | bytes 2359300
  1.8 0.7 copy-start.1
  2.5 0.7 copy-start.2
  3.2 0.7 copy-start.3
  3.9 0.7 copy-start.4

commit v4 on v3

--- a/solution.py
+++ b/solution.py
@@ -34,7 +34,7 @@
 def layer_kernel(
     hid_ref, gain_ref, lens_ref, pages_ref, freq_ref, wqkv_ref, wout_ref,
     out_ref, page_ref,
-    gathered, wbuf, acc, stats, columns, normed, table, qkv, qbuf, kv, keys, lows,
+    gathered, wbuf, acc, stats, columns, table, qkv, qbuf, kv, keys, lows,
     scores, peak, total, mix, done, heads, wo, x, sib_in, rx, hold, far_hold,
     w_sem, wo_sem, own_sem, stat_send, stat_recv, ici_send, ici_recv, sib_send, sib_recv,
     keep_sem, kv_send, kv_recv, q_send, q_recv, ag_send, ag_recv, o_send, o_recv,
@@ -61,8 +61,14 @@
     loads = {}
     for i, key in enumerate(shard_order):
         rows = pl.ds(pl.multiple_of(origin(*key) * SHARD, SHARD), SHARD)
-        loads[key] = pltpu.make_async_copy(wqkv_ref.at[:, rows, :], wbuf.at[:, rows, :], w_sem.at[i])
-        loads[key].start()
+        loads[key] = [
+            pltpu.make_async_copy(
+                wqkv_ref.at[kind, rows, :], wbuf.at[rows, kind * COLS:(kind + 1) * COLS], w_sem.at[i, kind]
+            )
+            for kind in range(3)
+        ]
+        for copy in loads[key]:
+            copy.start()
     own_copy = pltpu.make_async_copy(hid_ref, gathered.at[t], own_sem)
     own_copy.start()
     out_loads = {}
@@ -156,36 +162,28 @@
 
     def compute(key, half):
         who = origin(*key)
-
-        def normalise(i, carry):
-            rows = pl.ds(pl.multiple_of(half * HALF + i * 64, 64), 64)
-            here = pl.ds(pl.multiple_of(i * 64, 64), 64)
-            centre, scale = columns[0, rows, :], columns[1, rows, :]
-            for j in range(SHARD // 128):
+        rows = slice(half * HALF, (half + 1) * HALF)
+        product = None
+        for k in range(SHARD // HALF):
+            tiles = []
+            for j in range(2 * k, 2 * k + 2):
                 span = slice(128 * j, 128 * j + 128)
-                normed[here, span] = (
-                    (gathered[who, rows, span].astype(F32) - centre) * scale * gain_ref[who, :, span]
-                ).astype(BF16)
-            return carry
-
-        lax.fori_loop(0, HALF // 64, normalise, 0)
-        depth = pl.ds(pl.multiple_of(who * SHARD, SHARD), SHARD)
-        fresh = key == (0, 0)
-
-        def multiply(kind, carry):
-            product = jnp.dot(normed[...], wbuf[kind, depth, :], preferred_element_type=F32)
-            if fresh:
-                acc[kind] = product
-            else:
-                acc[kind] += product
-            return carry
-
-        lax.fori_loop(0, 3, multiply, 0)
+                tiles.append((
+                    (gathered[who, rows, span].astype(F32) - columns[0, rows, :])
+                    * columns[1, rows, :] * gain_ref[who, :, span]
+                ).astype(BF16))
+            depth = pl.ds(pl.multiple_of(who * SHARD + k * HALF, HALF), HALF)
+            term = jnp.dot(jnp.concatenate(tiles, axis=1), wbuf[depth, :], preferred_element_type=F32)
+            product = term if product is None else product + term
+        if key == (0, 0):
+            acc[...] = product
+        else:
+            acc[...] += product
 
     def epilogue(half):
         cosine, sine = table[half, 0], table[half, 1]
         for kind in range(3):
-            turned = jnp.transpose(acc[kind])
+            turned = jnp.transpose(acc[:, kind * COLS:(kind + 1) * COLS])
             for h in range(COLS // HD):
                 piece = turned[h * HD:(h + 1) * HD]
                 if kind < 2:
@@ -248,15 +246,19 @@
         minus[half][2].start()
         across[half][2].start()
 
+    def ready(key):
+        for copy in loads[key]:
+            copy.wait()
+
     own_copy.wait()
     for half in range(2):
         if half == 0:
-            loads[(0, 0)].wait()
+            ready((0, 0))
         compute((0, 0), half)
         relay_ring(half)
         if half == 0:
             send_own(1)
-            loads[(0, 1)].wait()
+            ready((0, 1))
         across[half][0].wait_recv()
         compute((0, 1), half)
         if half == 1:
@@ -266,36 +268,36 @@
         minus[half][1].wait_recv()
         across[half][4].start()
         if half == 0:
-            loads[(3, 0)].wait()
+            ready((3, 0))
         compute((3, 0), half)
         if half == 1:
             relay(0, 1)
         if half == 0:
-            loads[(1, 0)].wait()
+            ready((1, 0))
         compute((1, 0), half)
         if half == 1:
             relay(0, 2)
         across[half][1].wait_recv()
         across[half][3].wait_recv()
         if half == 0:
-            loads[(3, 1)].wait()
+            ready((3, 1))
         compute((3, 1), half)
         across[half][2].wait_recv()
         across[half][4].wait_recv()
         if half == 0:
-            loads[(1, 1)].wait()
+            ready((1, 1))
         compute((1, 1), half)
         plus[half][2].wait_recv()
         across[half][5].start()
         minus[half][2].wait_recv()
         across[half][6].start()
         if half == 0:
-            loads[(2, 0)].wait()
+            ready((2, 0))
         compute((2, 0), half)
         across[half][5].wait_recv()
         across[half][6].wait_recv()
         if half == 0:
-            loads[(2, 1)].wait()
+            ready((2, 1))
         compute((2, 1), half)
         epilogue(half)
         redistribute(half)
@@ -357,7 +359,8 @@
         oldest = 9 if k_half >= q_half else 8
         backs = list(range(newest, oldest))
 
-        def one(slot, carry):
+        def one(i, carry):
+            slot = (mine + 1 + i) % 4
             unit(slot, q_half, k_half, backs, k_half == 0)
             return carry
 
@@ -365,12 +368,16 @@
 
     o_copies = [[], []]
 
+    def finish(half, slot):
+        return (mix[half, slot] / total[half, slot]).astype(BF16)
+
     def give_back(half):
-        def one(slot, carry):
-            done[half, slot] = (mix[half, slot] / total[half, slot]).astype(BF16)
+        def one(i, carry):
+            slot = (mine + 1 + i) % 4
+            done[half, slot] = finish(half, slot)
             return carry
 
-        lax.fori_loop(0, 4, one, 0)
+        lax.fori_loop(0, 3, one, 0)
         for d in order:
             slot = (mine + d) % 4
             copy = remote(
@@ -379,7 +386,9 @@
             )
             copy.start()
             o_copies[half].append(copy)
-        heads[half, mine] = done[half, mine]
+
+    def keep(half):
+        heads[half, mine] = finish(half, mine)
 
     for copy in kept[0]:
         copy.wait()
@@ -418,8 +427,10 @@
     for copy in ag_copies[1]:
         copy.wait_recv()
     turn(1)
-    sweep(0, 1)
+    sweep(0, 1, 0, 3)
     give_back(0)
+    sweep(0, 1, 3, 4)
+    keep(0)
 
     rs_order = (2, 1, 3, 0)
     ring, across_sums = [{}, {}], [[], []]
@@ -495,9 +506,11 @@
         for copy in plus[half] + minus[half] + across[half]:
             copy.wait_send()
     first_part(0)
-    sweep(1, 1, 2, 4)
+    sweep(1, 1, 2, 3)
     give_back(1)
     second_part(0)
+    sweep(1, 1, 3, 4)
+    keep(1)
     first_part(1)
     last_part(0)
     second_part(1)
@@ -522,11 +535,10 @@
     frequency = jnp.asarray(np.repeat(frequency[:, None], 128, axis=1), F32)
     scratch = [
         pltpu.VMEM((8, ROWS, SHARD), BF16),
-        pltpu.VMEM((3, 8 * SHARD, COLS), BF16),
-        pltpu.VMEM((3, HALF, COLS), F32),
+        pltpu.VMEM((8 * SHARD, 3 * COLS), BF16),
+        pltpu.VMEM((HALF, 3 * COLS), F32),
         pltpu.VMEM((8, 8, ROWS), F32),
         pltpu.VMEM((2, ROWS, 128), F32),
-        pltpu.VMEM((HALF, SHARD), BF16),
         pltpu.VMEM((2, 2, ROT, HALF), F32),
         pltpu.VMEM((2, 4, 3, HD, HALF), BF16),
         pltpu.VMEM((2, 4, HD, HALF), BF16),
@@ -545,7 +557,7 @@
         pltpu.VMEM((2, 3, HALF, SHARD), BF16),
         pltpu.VMEM((2, 2, QUARTER, SHARD), F32),
         pltpu.VMEM((2, HALF, SHARD), F32),
-        DMA((8,)), DMA((8,)), DMA, DMA((7,)), DMA((7,)), DMA((2, 6)), DMA((2, 6)), DMA((2, 7)), DMA((2, 7)),
+        DMA((8, 3)), DMA((8,)), DMA, DMA((7,)), DMA((7,)), DMA((2, 6)), DMA((2, 6)), DMA((2, 7)), DMA((2, 7)),
         DMA((2, 2)), DMA((2, 3)), DMA((2, 3)), DMA((2, 3)), DMA((2, 3)), DMA((2, 4, 3)), DMA((2, 4, 3)),
         DMA((2, 3)), DMA((2, 3)), DMA((2, 4)), DMA((2, 4)), DMA((2, 6)), DMA((2, 6)),
     ]

time: 107 us -> 102 us (0.953)
  Pallas kernels: 100 us -> 95.8 us
    pallas_call x1, Pallas kernels: 100 us -> 95.8 us  [per_device(): pl.pallas_call(layer_kernel, out_shape=(jax.ShapeDtypeStruct((ROWS, SHARD...]
where the time goes in v4:
time: 102 us
  Pallas kernels  95.8 us (94%)
  local copies, waits for them, and re-layouts  5.64 us (6%)
    pallas_call x1, Pallas kernels, per_device(): pl.pallas_call(layer_kernel, out_shape=(jax.ShapeDtypeStruct((ROWS, SHARD...  95.8 us
    unnamed x12, local copies, waits for them, and re-layouts  5.64 us

profile of v4, /device:TPU:1, one launch (start us, length us, event | category | flops | bytes accessed | tf_op | source)
XLA Modules:
  0.0 102.1 jit_solution(15185606148366917183)
XLA Ops:
  0.6 0.0 copy-start
  0.6 1.1 %copy-done = bf16[512,768]{1,0:T(8,128)(2,1)S(1)} copy-done((bf16[512,768]{1,0:T(8,128)(2,1)S(1)}, bf16[512,768]{1,0:T(8,128)(2,1)}, u32[]{:S(2)}) %copy-start) | copy-done | bytes 786456
  1.8 0.0 copy-start.1
  1.8 0.7 copy-done.1
  2.5 0.0 copy-start.2
  2.5 0.7 copy-done.2
  3.2 0.0 copy-start.3
  3.2 0.7 copy-done.3
  3.9 0.0 copy-start.4
  3.9 0.7 copy-done.4
  4.5 95.8 %layer.1 = (bf16[512,768]{1,0:T(8,128)(2,1)S(1)}, bf16[2,32,16,384]{3,2,1,0:T(8,128)(2,1)S(1)}) custom-call(bf16[512,768]{1,0:T(8,128)(2,1)S(1)} %copy-done, f32[8,1,768]{2,1,0:T(1,128)S(1)} %bitcast.4, s32[1,64]{1,0:T(1,128)S(1)} %bitcast.5, s32[1,32]{1,0:T(1,128)S(1)} %bitcast.6, f32[24,128]{1,0:T(8,128)S(1)} %copy-done.2, bf16[3,6144,384]{2,1,0:T(8,128)(2,1)} %bitcast.7, ...), custom_call_target="tpu_custom_call" | custom-call | tf_op jit(solution)/shard_map/layer/pallas_call | solution.py:564
  100.3 0.9 copy.11
  101.2 0.9 copy.12
Async XLA Ops:
  0.6 1.1 %copy-start = (bf16[512,768]{1,0:T(8,128)(2,1)S(1)}, bf16[512,768]{1,0:T(8,128)(2,1)}, u32[]{:S(2)}) copy-start(bf16[512,768]{1,0:T(8,128)(2,1)} %hid_ref.1) | copy-start | bytes 2359300
  1.8 0.7 copy-start.1
  2.5 0.7 copy-start.2
  3.2 0.7 copy-start.3
  3.9 0.7 copy-start.4

commit v5 on v4

--- a/solution.py
+++ b/solution.py
@@ -32,11 +32,11 @@
 
 
 def layer_kernel(
-    hid_ref, gain_ref, lens_ref, pages_ref, freq_ref, wqkv_ref, wout_ref,
+    hid_hbm, gain_hbm, lens_hbm, pages_hbm, freq_hbm, wqkv_ref, wout_ref,
     out_ref, page_ref,
-    gathered, wbuf, acc, stats, columns, table, qkv, qbuf, kv, keys, lows,
+    gain_ref, lens_ref, pages_ref, freq_ref, gathered, wbuf, acc, stats, columns, table, qkv, qbuf, kv, keys, lows,
     scores, peak, total, mix, done, heads, wo, x, sib_in, rx, hold, far_hold,
-    w_sem, wo_sem, own_sem, stat_send, stat_recv, ici_send, ici_recv, sib_send, sib_recv,
+    w_sem, wo_sem, own_sem, small_sem, stat_send, stat_recv, ici_send, ici_recv, sib_send, sib_recv,
     keep_sem, kv_send, kv_recv, q_send, q_recv, ag_send, ag_recv, o_send, o_recv,
     give_send, give_recv, ring_send, ring_recv,
 ):
@@ -57,6 +57,24 @@
     def origin(dz, k):
         return ((z + dz) % 4) * 2 + (c + k) % 2
 
+    barrier = pltpu.get_barrier_semaphore()
+    for d in range(1, 8):
+        pl.semaphore_signal(barrier, inc=1, device_id=(b, (t + d) % 8), device_id_type=MESH)
+    for d in range(1, 4):
+        for where in (block_of((mine + d) % 4, group), block_of(mine, (group + d) % 4)):
+            pl.semaphore_signal(barrier, inc=1, device_id=(where, t), device_id_type=MESH)
+
+    own_copy = pltpu.make_async_copy(hid_hbm, gathered.at[t], own_sem)
+    own_copy.start()
+    small = [
+        pltpu.make_async_copy(src, dst, small_sem.at[i])
+        for i, (src, dst) in enumerate(
+            [(lens_hbm, lens_ref), (freq_hbm, freq_ref), (gain_hbm, gain_ref), (pages_hbm, pages_ref)]
+        )
+    ]
+    for copy in small:
+        copy.start()
+
     shard_order = [(0, 0), (0, 1), (3, 0), (1, 0), (3, 1), (1, 1), (2, 0), (2, 1)]
     loads = {}
     for i, key in enumerate(shard_order):
@@ -69,8 +87,6 @@
         ]
         for copy in loads[key]:
             copy.start()
-    own_copy = pltpu.make_async_copy(hid_ref, gathered.at[t], own_sem)
-    own_copy.start()
     out_loads = {}
     for i, key in enumerate([(2, 1), (2, 0), (1, 1), (1, 0), (3, 1), (3, 0), (0, 1), (0, 0)]):
         who = origin(*key)
@@ -78,14 +94,8 @@
         out_loads[key] = pltpu.make_async_copy(wout_ref.at[:, span], wo.at[who], wo_sem.at[i])
         out_loads[key].start()
 
-    barrier = pltpu.get_barrier_semaphore()
-    for d in range(1, 8):
-        pl.semaphore_signal(barrier, inc=1, device_id=(b, (t + d) % 8), device_id_type=MESH)
-    for d in range(1, 4):
-        for where in (block_of((mine + d) % 4, group), block_of(mine, (group + d) % 4)):
-            pl.semaphore_signal(barrier, inc=1, device_id=(where, t), device_id_type=MESH)
-
-    value = hid_ref[...].astype(F32)
+    own_copy.wait()
+    value = gathered[t].astype(F32)
     mean = jnp.sum(value, axis=1, keepdims=True) * (1.0 / SHARD)
     centred = value - mean
     spread = jnp.sum(centred * centred, axis=1, keepdims=True)
@@ -111,15 +121,15 @@
             return remote(src.at[rows], gathered.at[who, rows], ici_send.at[half, i], ici_recv.at[half, i], where)
 
         plus.append([
-            ici(0, t, q0, hid_ref, after), ici(1, t, q1, hid_ref, after), ici(2, left, q0, gathered.at[left], after),
+            ici(0, t, q0, gathered.at[t], after), ici(1, t, q1, gathered.at[t], after), ici(2, left, q0, gathered.at[left], after),
         ])
         minus.append([
-            ici(3, t, q1, hid_ref, before), ici(4, t, q0, hid_ref, before), ici(5, right, q1, gathered.at[right], before),
+            ici(3, t, q1, gathered.at[t], before), ici(4, t, q0, gathered.at[t], before), ici(5, right, q1, gathered.at[right], before),
         ])
         moved = [(t, both), (left, q0), (right, q1), (left, q1), (right, q0), (far, q0), (far, q1)]
         across.append([
             remote(
-                (hid_ref if i == 0 else gathered.at[who]).at[rows], gathered.at[who, rows],
+                gathered.at[who, rows], gathered.at[who, rows],
                 sib_send.at[half, i], sib_recv.at[half, i], sibling,
             )
             for i, (who, rows) in enumerate(moved)
@@ -134,6 +144,8 @@
 
     send_own(0)
 
+    for copy in small:
+        copy.wait()
     lens = lens_ref[...].astype(F32)
     earlier = iota((64, 64), 1) < iota((64, 64), 0)
     starts = jnp.sum(jnp.where(earlier, lens, 0.0), axis=1, keepdims=True)
@@ -250,7 +262,6 @@
         for copy in loads[key]:
             copy.wait()
 
-    own_copy.wait()
     for half in range(2):
         if half == 0:
             ready((0, 0))
@@ -526,7 +537,7 @@
 
 
 VMEM = pl.BlockSpec(memory_space=pltpu.VMEM)
-ANY = pl.BlockSpec(memory_space=pl.ANY)
+HBM = pl.BlockSpec(memory_space=pltpu.MemorySpace.HBM)
 DMA = pltpu.SemaphoreType.DMA
 
 
@@ -534,6 +545,10 @@
     frequency = 10000.0 ** (-(2.0 * (np.arange(ROT) % (ROT // 2))) / ROT)
     frequency = jnp.asarray(np.repeat(frequency[:, None], 128, axis=1), F32)
     scratch = [
+        pltpu.VMEM((8, 1, SHARD), F32),
+        pltpu.VMEM((1, 64), jnp.int32),
+        pltpu.VMEM((1, 32), jnp.int32),
+        pltpu.VMEM((ROT, 128), F32),
         pltpu.VMEM((8, ROWS, SHARD), BF16),
         pltpu.VMEM((8 * SHARD, 3 * COLS), BF16),
         pltpu.VMEM((HALF, 3 * COLS), F32),
@@ -557,7 +572,7 @@
         pltpu.VMEM((2, 3, HALF, SHARD), BF16),
         pltpu.VMEM((2, 2, QUARTER, SHARD), F32),
         pltpu.VMEM((2, HALF, SHARD), F32),
-        DMA((8, 3)), DMA((8,)), DMA, DMA((7,)), DMA((7,)), DMA((2, 6)), DMA((2, 6)), DMA((2, 7)), DMA((2, 7)),
+        DMA((8, 3)), DMA((8,)), DMA, DMA((4,)), DMA((7,)), DMA((7,)), DMA((2, 6)), DMA((2, 6)), DMA((2, 7)), DMA((2, 7)),
         DMA((2, 2)), DMA((2, 3)), DMA((2, 3)), DMA((2, 3)), DMA((2, 3)), DMA((2, 4, 3)), DMA((2, 4, 3)),
         DMA((2, 3)), DMA((2, 3)), DMA((2, 4)), DMA((2, 4)), DMA((2, 6)), DMA((2, 6)),
     ]
@@ -567,17 +582,20 @@
             jax.ShapeDtypeStruct((ROWS, SHARD), BF16),
             jax.ShapeDtypeStruct((2, ROWS // PAGE, PAGE, COLS), BF16),
         ),
-        in_specs=[VMEM] * 5 + [ANY] * 2,
+        in_specs=[HBM] * 7,
         out_specs=(VMEM, VMEM),
         scratch_shapes=scratch,
         compiler_params=pltpu.CompilerParams(
             collective_id=0, has_side_effects=True, vmem_limit_bytes=49 * 1024 * 1024
         ),
         name="layer",
-    )(
-        hidden_in, ln_gain.reshape(8, 1, SHARD), doc_lengths.reshape(1, 64), page_table.reshape(1, 32), frequency,
-        jnp.transpose(w_qkv, (1, 0, 2)), w_out,
-    )
+    )(*[
+        pltpu.with_memory_space_constraint(operand, pltpu.MemorySpace.HBM)
+        for operand in (
+            hidden_in, ln_gain.reshape(8, 1, SHARD), doc_lengths.reshape(1, 64), page_table.reshape(1, 32), frequency,
+            jnp.transpose(w_qkv, (1, 0, 2)), w_out,
+        )
+    ])
     return attn_out, pages
 
 

time: 102 us -> 103 us (level)
  Pallas kernels: 95.8 us -> 100 us
  local copies, waits for them, and re-layouts: 5.64 us -> 1.76 us
    pallas_call x1, Pallas kernels: 95.8 us -> 100 us  [per_device(): pl.pallas_call(layer_kernel, out_shape=(jax.ShapeDtypeStruct((ROWS, SHARD...]
    unnamed x12 -> x2, local copies, waits for them, and re-layouts: 5.64 us -> 1.76 us
where the time goes in v5:
time: 103 us
  Pallas kernels  100 us (97%)
  local copies, waits for them, and re-layouts  1.76 us (2%)
    pallas_call x1, Pallas kernels, per_device(): pl.pallas_call(layer_kernel, out_shape=(jax.ShapeDtypeStruct((ROWS, SHARD...  100 us

profile of v5, /device:TPU:1, one launch (start us, length us, event | category | flops | bytes accessed | tf_op | source)
XLA Modules:
  0.0 102.9 jit_solution(15657590117646948213)
XLA Ops:
  0.6 100.5 %layer.1 = (bf16[512,768]{1,0:T(8,128)(2,1)S(1)}, bf16[2,32,16,384]{3,2,1,0:T(8,128)(2,1)S(1)}) custom-call(bf16[512,768]{1,0:T(8,128)(2,1)} %hid_hbm.1, f32[8,1,768]{2,1,0:T(1,128)} %bitcast.5, s32[1,64]{1,0:T(1,128)} %bitcast.6, s32[1,32]{1,0:T(1,128)} %bitcast.7, f32[24,128]{1,0:T(8,128)} %constant.2.clone.freq_hbm, bf16[3,6144,384]{2,1,0:T(8,128)(2,1)} %bitcast.4, ...), custom_call_target="tpu_custom_call" | custom-call | tf_op jit(solution)/shard_map/layer/pallas_call | solution.py:579
  101.1 0.9 copy.11
  102.0 0.9 copy.12

commit v6 on v5

--- a/solution.py
+++ b/solution.py
@@ -85,16 +85,21 @@
             )
             for kind in range(3)
         ]
-        for copy in loads[key]:
-            copy.start()
     out_loads = {}
     for i, key in enumerate([(2, 1), (2, 0), (1, 1), (1, 0), (3, 1), (3, 0), (0, 1), (0, 0)]):
         who = origin(*key)
         span = pl.ds(pl.multiple_of(who * SHARD, SHARD), SHARD)
         out_loads[key] = pltpu.make_async_copy(wout_ref.at[:, span], wo.at[who], wo_sem.at[i])
-        out_loads[key].start()
+
+    def fetch(wanted):
+        for key in wanted:
+            for copy in loads[key]:
+                copy.start()
 
     own_copy.wait()
+    for copy in small:
+        copy.wait()
+    fetch(shard_order[:2])
     value = gathered[t].astype(F32)
     mean = jnp.sum(value, axis=1, keepdims=True) * (1.0 / SHARD)
     centred = value - mean
@@ -143,9 +148,8 @@
         minus[half][1].start()
 
     send_own(0)
-
-    for copy in small:
-        copy.wait()
+    fetch(shard_order[2:])
+
     lens = lens_ref[...].astype(F32)
     earlier = iota((64, 64), 1) < iota((64, 64), 0)
     starts = jnp.sum(jnp.where(earlier, lens, 0.0), axis=1, keepdims=True)
@@ -270,6 +274,9 @@
         if half == 0:
             send_own(1)
             ready((0, 1))
+        else:
+            for copy in out_loads.values():
+                copy.start()
         across[half][0].wait_recv()
         compute((0, 1), half)
         if half == 1:

time: 103 us -> 98.6 us (0.957)
  Pallas kernels: 100 us -> 96.1 us
    pallas_call x1, Pallas kernels: 100 us -> 96.1 us  [per_device(): pl.pallas_call(layer_kernel, out_shape=(jax.ShapeDtypeStruct((ROWS, SHARD...]
where the time goes in v6:
time: 98.6 us; the launch traced here: 98.5 us
  Pallas kernels  96.1 us (97%)
  local copies, waits for them, and re-layouts  1.76 us (2%)
    pallas_call x1, Pallas kernels, per_device(): pl.pallas_call(layer_kernel, out_shape=(jax.ShapeDtypeStruct((ROWS, SHARD...  96.1 us

profile of v6, /device:TPU:1, one launch (start us, length us, event | category | flops | bytes accessed | tf_op | source)
XLA Modules:
  0.0 98.5 jit_solution(1210568274380110016)
XLA Ops:
  0.6 96.1 %layer.1 = (bf16[512,768]{1,0:T(8,128)(2,1)S(1)}, bf16[2,32,16,384]{3,2,1,0:T(8,128)(2,1)S(1)}) custom-call(bf16[512,768]{1,0:T(8,128)(2,1)} %hid_hbm.1, f32[8,1,768]{2,1,0:T(1,128)} %bitcast.5, s32[1,64]{1,0:T(1,128)} %bitcast.6, s32[1,32]{1,0:T(1,128)} %bitcast.7, f32[24,128]{1,0:T(8,128)} %constant.2.clone.freq_hbm, bf16[3,6144,384]{2,1,0:T(8,128)(2,1)} %bitcast.4, ...), custom_call_target="tpu_custom_call" | custom-call | tf_op jit(solution)/shard_map/layer/pallas_call | solution.py:586
  96.7 0.9 copy.11
  97.6 0.9 copy.12

commit v7 on v6

--- a/solution.py
+++ b/solution.py
@@ -442,9 +442,15 @@
             moved = term if moved is None else moved + term
         page_ref[kind] = moved.astype(BF16).reshape(ROWS // PAGE, PAGE, COLS)
 
-    for copy in ag_copies[1]:
+    def turn_one(g, a):
+        keys[1, g, a] = jnp.transpose(kv[1, g, a, 0].astype(F32)).astype(BF16)
+
+    for a in range(4):
+        turn_one(group, a)
+    for n, copy in enumerate(ag_copies[1]):
         copy.wait_recv()
-    turn(1)
+        d = order[n // 3 - 1] if n >= 3 else 0
+        turn_one((group + 4 - order[n % 3]) % 4, (mine + 4 - d) % 4)
     sweep(0, 1, 0, 3)
     give_back(0)
     sweep(0, 1, 3, 4)

time: 98.6 us -> 96.9 us (0.983)
  Pallas kernels: 96.1 us -> 94.4 us
    pallas_call x1, Pallas kernels: 96.1 us -> 94.4 us  [per_device(): pl.pallas_call(layer_kernel, out_shape=(jax.ShapeDtypeStruct((ROWS, SHARD...]
where the time goes in v7:
time: 96.9 us; the launch traced here: 96.8 us
  Pallas kernels  94.4 us (97%)
  local copies, waits for them, and re-layouts  1.76 us (2%)
    pallas_call x1, Pallas kernels, per_device(): pl.pallas_call(layer_kernel, out_shape=(jax.ShapeDtypeStruct((ROWS, SHARD...  94.4 us

profile of v7, /device:TPU:1, one launch (start us, length us, event | category | flops | bytes accessed | tf_op | source)
XLA Modules:
  0.0 96.8 jit_solution(8884480902762519271)
XLA Ops:
  0.6 94.4 %layer.1 = (bf16[512,768]{1,0:T(8,128)(2,1)S(1)}, bf16[2,32,16,384]{3,2,1,0:T(8,128)(2,1)S(1)}) custom-call(bf16[512,768]{1,0:T(8,128)(2,1)} %hid_hbm.1, f32[8,1,768]{2,1,0:T(1,128)} %bitcast.5, s32[1,64]{1,0:T(1,128)} %bitcast.6, s32[1,32]{1,0:T(1,128)} %bitcast.7, f32[24,128]{1,0:T(8,128)} %constant.2.clone.freq_hbm, bf16[3,6144,384]{2,1,0:T(8,128)(2,1)} %bitcast.4, ...), custom_call_target="tpu_custom_call" | custom-call | tf_op jit(solution)/shard_map/layer/pallas_call | solution.py:592
  95.0 0.9 copy.11
  95.9 0.9 copy.12
